TPU v7x, 32 devices: a whole 2x2x4 slice. The times are simulated.
32 devices in a mesh: ha: 2 (over core), wa: 4 (over y, x), ba: 4 (over z).
Axes of the slice: x: 2, y: 2, z: 4, core: 2. Of those that a mesh axis runs over, the one named last changes fastest.
Arguments:
- images: bfloat16 [168, 24, 24, 384], P('ba', 'ha', 'wa'), may hold values from -6 to 6
- out_grad: bfloat16 [168, 24, 24, 384], P('ba', 'ha', 'wa'), may hold values from -6 to 6
- keep_mask: int32 [168], P('ba'), may hold values 0 or 1
- img_counts: int32 [4], P('ba'), may hold values from 1 to 42, 87 in all
- mats_master: float32 [2, 384, 1536], P(None, None, 'ba'), may hold values from -0.3125 to 0.3125
- chan_master: float32 [54, 384], P(None, 'ba')
- bias_master: float32 [1536], P('ba'), may hold values from -3 to 3
- mats_moment: float32 [2, 384, 1536], P(None, None, 'ba'), may hold values from -1024 to 1024
- chan_moment: float32 [54, 384], P(None, 'ba'), may hold values from -1024 to 1024
- bias_moment: float32 [1536], P('ba'), may hold values from -1024 to 1024
- mats_second: float32 [2, 384, 1536], P(None, None, 'ba'), may hold values from 34836.48 to 139345.92
- chan_second: float32 [54, 384], P(None, 'ba'), may hold values from 34836.48 to 139345.92
- bias_second: float32 [1536], P('ba'), may hold values from 34836.48 to 139345.92
- mats_average: float32 [2, 384, 1536], P(None, None, 'ba'), may hold values from -0.3125 to 0.3125
- chan_average: float32 [54, 384], P(None, 'ba')
- bias_average: float32 [1536], P('ba'), may hold values from -3 to 3
Outputs:
- outputs: bfloat16 [168, 24, 24, 384], P('ba', 'ha', 'wa')
- input_grad: bfloat16 [168, 24, 24, 384], P('ba', 'ha', 'wa')
- mats_grad: float32 [2, 384, 1536], P(None, None, 'ba')
- chan_grad: float32 [54, 384], P(None, 'ba')
- bias_grad: float32 [1536], P('ba')
- mats_new: float32 [2, 384, 1536], P(None, None, 'ba')
- chan_new: float32 [54, 384], P(None, 'ba')
- bias_new: float32 [1536], P('ba')
- mats_moment_new: float32 [2, 384, 1536], P(None, None, 'ba')
- chan_moment_new: float32 [54, 384], P(None, 'ba')
- bias_moment_new: float32 [1536], P('ba')
- mats_second_new: float32 [2, 384, 1536], P(None, None, 'ba')
- chan_second_new: float32 [54, 384], P(None, 'ba')
- bias_second_new: float32 [1536], P('ba')
- mats_average_new: float32 [2, 384, 1536], P(None, None, 'ba')
- chan_average_new: float32 [54, 384], P(None, 'ba')
- bias_average_new: float32 [1536], P('ba')
- mats_low: bfloat16 [2, 384, 1536], P(None, None, 'ba')
- chan_low: bfloat16 [54, 384], P(None, 'ba')
- bias_low: bfloat16 [1536], P('ba')
Inputs may be any that keep to these rules, and one draw needn't show every extreme that they name: `img_counts`: one index of ba holds exactly 42 filled slots.
All inputs are finite; a program needn't handle non-finite values. No bound on the sum of `keep_mask` or of `img_counts` on one device may be relied on, other than what follows from the above.
Results may differ from a plain program's by a relative error of at most 0.0098.
Values may be sent and summed in bfloat16 or wider, within the bound.
A program may use at most 192 MiB of HBM per device.

v0:
```python
import jax
import jax.numpy as jnp
from jax import lax
from jax.sharding import PartitionSpec as P

C = 384
KS = 7
STEP = 3


def with_halo(cells, sides, width):
    for axis, dim in sides:
        count = lax.axis_size(axis)
        ends = count - 1
        head = lax.slice_in_dim(cells, 0, width, axis=dim)
        tail = lax.slice_in_dim(cells, cells.shape[dim] - width, cells.shape[dim], axis=dim)
        cells = jnp.concatenate(
            [
                lax.ppermute(tail, axis, [(i, (i + 1) % count) for i in range(ends)]),
                cells,
                lax.ppermute(head, axis, [((i + 1) % count, i) for i in range(ends)]),
            ],
            axis=dim,
        )
    return cells


def exact_gelu(value):
    return jax.nn.gelu(value, approximate=False)


def depthwise(padded, taps, tile_rows, tile_cols, flipped):
    total = jnp.zeros((padded.shape[0], tile_rows, tile_cols, padded.shape[3]), jnp.float32)
    for i in range(KS):
        for j in range(KS):
            if flipped:
                piece = padded[
                    :, KS - 1 - i : KS - 1 - i + tile_rows, KS - 1 - j : KS - 1 - j + tile_cols, :
                ]
            else:
                piece = padded[:, i : i + tile_rows, j : j + tile_cols, :]
            total = total + piece.astype(jnp.float32) * taps[i * KS + j]
    return total


def adam_step(master, grad, moment, second, average, rate):
    moment_new = 0.5 * moment + 0.5 * grad
    second_new = 0.5 * second + 0.5 * grad * grad
    correct = 1.0 - 0.5**STEP
    master_new = master - rate * (
        moment_new / correct / (jnp.sqrt(second_new / correct) + 1e-08) + 0.05 * master
    )
    average_new = 0.9 * average + 0.1 * master_new
    return (master_new, moment_new, second_new, average_new)


def local(
    images,
    out_grad,
    keep_mask,
    img_counts,
    mats_master,
    chan_master,
    bias_master,
    mats_moment,
    chan_moment,
    bias_moment,
    mats_second,
    chan_second,
    bias_second,
    mats_average,
    chan_average,
    bias_average,
):
    reach = KS // 2
    first = KS * KS
    mats_all, chan_all, bias_all = (
        lax.all_gather(mats_master.astype(jnp.bfloat16), "ba", axis=2, tiled=True),
        lax.all_gather(chan_master.astype(jnp.bfloat16), "ba", axis=1, tiled=True),
        lax.all_gather(bias_master.astype(jnp.bfloat16), "ba", axis=0, tiled=True),
    )
    w_in = mats_all[0]
    w_out = mats_all[1]
    chan_vals = chan_all.astype(jnp.float32)
    taps = chan_vals[:first]
    conv_bias = chan_vals[first]
    gain = chan_vals[first + 1]
    shift = chan_vals[first + 2]
    out_bias = chan_vals[first + 3]
    scale = chan_vals[first + 4]
    hid_bias = bias_all.astype(jnp.float32)
    slot_count, tile_rows, tile_cols = (images.shape[0], images.shape[1], images.shape[2])
    slots = jnp.arange(slot_count, dtype=jnp.int32) < img_counts[0]
    gate = jnp.where(slots, keep_mask, 0).astype(jnp.float32)[:, None, None, None]
    padded = with_halo(images, (("ha", 1), ("wa", 2)), reach)
    conv = depthwise(padded, taps, tile_rows, tile_cols, False) + conv_bias
    center = conv - jnp.mean(conv, axis=-1, keepdims=True)
    inverse = lax.rsqrt(jnp.mean(center * center, axis=-1, keepdims=True) + 1e-06)
    normed = center * inverse
    flat_in = (normed * gain + shift).astype(jnp.bfloat16).reshape(-1, C)
    hidden_pre = jnp.dot(flat_in, w_in, preferred_element_type=jnp.float32) + hid_bias
    activated, gelu_pull = jax.vjp(exact_gelu, hidden_pre)
    act_low = activated.astype(jnp.bfloat16)
    branch = (
        lax.dot_general(
            act_low, w_out, (((1,), (1,)), ((), ())), preferred_element_type=jnp.float32
        )
        + out_bias
    )
    branch = branch.reshape(images.shape)
    outputs = (images.astype(jnp.float32) + gate * scale * branch).astype(jnp.bfloat16)
    upstream = out_grad.astype(jnp.float32)
    branch_grad = (gate * scale * upstream).astype(jnp.bfloat16)
    grad_scale = jnp.sum(gate * upstream * branch, axis=(0, 1, 2))
    flat_branch = branch_grad.reshape(-1, C)
    grad_outb = jnp.sum(flat_branch, axis=0, dtype=jnp.float32)
    grad_wout = lax.dot_general(
        flat_branch, act_low, (((0,), (0,)), ((), ())), preferred_element_type=jnp.float32
    )
    act_grad = jnp.dot(flat_branch, w_out, preferred_element_type=jnp.float32)
    pre_grad = gelu_pull(act_grad)[0].astype(jnp.bfloat16)
    grad_hbias = jnp.sum(pre_grad, axis=0, dtype=jnp.float32)
    grad_win = lax.dot_general(
        flat_in, pre_grad, (((0,), (0,)), ((), ())), preferred_element_type=jnp.float32
    )
    normed_grad = lax.dot_general(
        pre_grad, w_in, (((1,), (1,)), ((), ())), preferred_element_type=jnp.float32
    ).reshape(images.shape)
    grad_gain = jnp.sum(normed_grad * normed, axis=(0, 1, 2))
    grad_shift = jnp.sum(normed_grad, axis=(0, 1, 2))
    scaled = normed_grad * gain
    conv_grad = inverse * (
        scaled
        - jnp.mean(scaled, axis=-1, keepdims=True)
        - normed * jnp.mean(scaled * normed, axis=-1, keepdims=True)
    )
    conv_grad = conv_grad.astype(jnp.bfloat16)
    grad_cbias = jnp.sum(conv_grad, axis=(0, 1, 2), dtype=jnp.float32)
    tap_rows = []
    for i in range(KS):
        for j in range(KS):
            piece = padded[:, i : i + tile_rows, j : j + tile_cols, :].astype(jnp.float32)
            tap_rows.append(jnp.sum(piece * conv_grad.astype(jnp.float32), axis=(0, 1, 2)))
    grad_taps = jnp.stack(tap_rows, axis=0)
    grad_padded = with_halo(conv_grad, (("ha", 1), ("wa", 2)), reach)
    input_grad = (upstream + depthwise(grad_padded, taps, tile_rows, tile_cols, True)).astype(
        jnp.bfloat16
    )
    mats_local = jnp.stack([grad_win, grad_wout], axis=0)
    chan_local = jnp.concatenate(
        [grad_taps, jnp.stack([grad_cbias, grad_gain, grad_shift, grad_outb, grad_scale], axis=0)],
        axis=0,
    )
    whole = lax.psum((mats_local, chan_local, grad_hbias), ("ha", "wa"))
    mats_grad, chan_grad, bias_grad = (
        lax.psum_scatter(whole[0], "ba", scatter_dimension=2, tiled=True),
        lax.psum_scatter(whole[1], "ba", scatter_dimension=1, tiled=True),
        lax.psum_scatter(whole[2], "ba", scatter_dimension=0, tiled=True),
    )
    mats_new, mats_moment_new, mats_second_new, mats_average_new = adam_step(
        mats_master, mats_grad, mats_moment, mats_second, mats_average, 0.03
    )
    chan_new, chan_moment_new, chan_second_new, chan_average_new = adam_step(
        chan_master, chan_grad, chan_moment, chan_second, chan_average, 0.3
    )
    bias_new, bias_moment_new, bias_second_new, bias_average_new = adam_step(
        bias_master, bias_grad, bias_moment, bias_second, bias_average, 0.3
    )
    return (
        outputs,
        input_grad,
        mats_grad,
        chan_grad,
        bias_grad,
        mats_new,
        chan_new,
        bias_new,
        mats_moment_new,
        chan_moment_new,
        bias_moment_new,
        mats_second_new,
        chan_second_new,
        bias_second_new,
        mats_average_new,
        chan_average_new,
        bias_average_new,
        mats_new.astype(jnp.bfloat16),
        chan_new.astype(jnp.bfloat16),
        bias_new.astype(jnp.bfloat16),
    )


def solution(mesh):
    return jax.shard_map(
        local,
        mesh=mesh,
        in_specs=(
            P("ba", "ha", "wa", None),
            P("ba", "ha", "wa", None),
            P("ba"),
            P("ba"),
            P(None, None, "ba"),
            P(None, "ba"),
            P("ba"),
            P(None, None, "ba"),
            P(None, "ba"),
            P("ba"),
            P(None, None, "ba"),
            P(None, "ba"),
            P("ba"),
            P(None, None, "ba"),
            P(None, "ba"),
            P("ba"),
        ),
        out_specs=(
            P("ba", "ha", "wa", None),
            P("ba", "ha", "wa", None),
            P(None, None, "ba"),
            P(None, "ba"),
            P("ba"),
            P(None, None, "ba"),
            P(None, "ba"),
            P("ba"),
            P(None, None, "ba"),
            P(None, "ba"),
            P("ba"),
            P(None, None, "ba"),
            P(None, "ba"),
            P("ba"),
            P(None, None, "ba"),
            P(None, "ba"),
            P("ba"),
            P(None, None, "ba"),
            P(None, "ba"),
            P("ba"),
        ),
        check_vma=False,
    )
```

profile of v0, /device:TPU:0, one launch (start us, length us, event | category | flops | bytes accessed | tf_op | source)
XLA Modules:
  0.0 585.8 jit_solution(15052073042817741762)
XLA Ops:
  28.3 12.1 %all-gather.1 = bf16[4,1,384]{2,1,0:T(2,128)(2,1)S(1)} all-gather(bf16[1,1,384]{2,1,0:T(2,128)(2,1)S(1)} %reshape.160), channel_id=1, replica_groups=mesh['ha'=2,'wa'=4,'ba'=4] {'ba'}, dimensions={0}, use_global_device_ids=true | all-gather | bytes 3840 | tf_op jit(solution)/shard_map/all_gather | solution.py:80
  40.5 14.2 %all-gather = bf16[4,96,54]{1,2,0:T(8,128)(2,1)S(1)} all-gather(bf16[1,96,54]{1,2,0:T(8,128)(2,1)S(1)} %convert_bitcast_fusion), channel_id=1, replica_groups=mesh['ha'=2,'wa'=4,'ba'=4] {'ba'}, dimensions={0}, use_global_device_ids=true | all-gather | bytes 51840 | tf_op jit(solution)/shard_map/all_gather | solution.py:79
  58.0 9.7 %collective-permute-done.2 = bf16[42,18,3,384]{3,0,2,1:T(8,128)(2,1)} collective-permute-done((bf16[42,18,3,384]{3,0,2,1:T(8,128)(2,1)}, bf16[42,18,3,384]{3,0,2,1:T(8,128)(2,1)}, u32[]{:S(2)}, u32[]{:S(2)}) %collective-permute-start.2) | collective-permute-done | bytes 1741856 | tf_op jit(solution)/shard_map/ppermute | solution.py:19
  67.6 44.6 %collective-permute-done.3 = bf16[42,18,3,384]{3,0,2,1:T(8,128)(2,1)} collective-permute-done((bf16[42,18,3,384]{3,0,2,1:T(8,128)(2,1)}, bf16[42,18,3,384]{3,0,2,1:T(8,128)(2,1)}, u32[]{:S(2)}, u32[]{:S(2)}) %collective-permute-start.3) | collective-permute-done | bytes 1741856 | tf_op jit(solution)/shard_map/ppermute | solution.py:21
  112.2 59.9 %fusion.197 = (f32[42,12,6]{0,2,1:T(8,128)S(1)}, f32[42,12,6,384]{3,0,2,1:T(8,128)S(1)}) fusion(f32[384]{0:T(512)S(1)} %get-tuple-element.85, f32[384]{0:T(512)S(1)} %get-tuple-element.86, bf16[42,18,3,384]{3,0,2,1:T(8,128)(2,1)} %collective-permute-done.3, bf16[42,18,6,384]{3,0,2,1:T(8,128)(2,1)} %copy-done, f32[384]{0:T(512)S(1)} %get-tuple-element.87, ...), kind=kLoop, calls=%fused_computation.497 | loop fusion | flops 220628016 | bytes 27958080 | tf_op jit(solution)/shard_map/reduce_sum | solution.py:97
  182.2 46.0 %multiply_convert_fusion = (bf16[3024,1536]{1,0:T(8,128)(2,1)S(1)}, f32[3024,1536]{1,0:T(8,128)}, f32[3024,1536]{1,0:T(8,128)}) fusion(f32[1536]{0:T(1024)S(1)} %reshape.162, bf16[3024,384]{1,0:T(8,128)(2,1)S(1)} %reshape.155, bf16[2,384,1536]{2,1,0:T(8,128)(2,1)} %all-gather.4.cloned.1.call-done), kind=kOutput, calls=%fused_computation.95 | convolution fusion | flops 3873816576 | bytes 49956864 | tf_op jit(solution)/shard_map/dot_general | solution.py:101
  231.6 7.1 %convolution_add_fusion = f32[3024,384]{1,0:T(8,128)} fusion(bf16[3024,1536]{1,0:T(8,128)(2,1)S(1)} %get-tuple-element.152, f32[384]{0:T(512)S(1)} %copy-done.114, bf16[2,384,1536]{2,1,0:T(8,128)(2,1)S(1)} %copy-done.115), kind=kOutput, calls=%fused_computation.347 | convolution fusion | flops 3568416768 | bytes 15116288 | tf_op jit(solution)/shard_map/dot_general | solution.py:105
  238.8 6.7 %reshape.156 = f32[42,12,6,384]{3,2,1,0:T(8,128)} reshape(f32[3024,384]{1,0:T(8,128)} %convolution_add_fusion) | data formatting | bytes 9289728 | tf_op jit(solution)/shard_map/reshape | solution.py:110
  258.0 8.7 %convolution_bitcast_fusion = f32[1,384,1536]{2,1,0:T(8,128)} fusion(bf16[3024,384]{1,0:T(8,128)(2,1)S(1)} %reshape.157, bf16[3024,1536]{1,0:T(8,128)(2,1)} %copy-done.10), kind=kOutput, calls=%fused_computation.353 | convolution fusion | flops 3567255552 | bytes 13971456 | tf_op jit(solution)/shard_map/dot_general | solution.py:117
  266.7 22.9 %convert_reduce_fusion.1 = (f32[1536]{0:T(1024)S(1)}, bf16[3024,1536]{1,0:T(8,128)(2,1)}) fusion(f32[3024,1536]{1,0:T(8,128)} %get-tuple-element.153, bf16[3024,384]{1,0:T(8,128)(2,1)} %copy-done.13, bf16[2,384,1536]{2,1,0:T(8,128)(2,1)} %all-gather.4.cloned.1.call-done, f32[3024,1536]{1,0:T(8,128)} %get-tuple-element.177, f32[1536]{0:T(1024)S(1)} %reshape.162), kind=kOutput, calls=%fused_computation.93 | convolution fusion | flops 3646216704 | bytes 49963008 | tf_op jit(solution)/shard_map/dot_general | solution.py:120
  289.6 7.8 %convolution_bitcast_fusion.1 = f32[1,384,1536]{2,1,0:T(8,128)} fusion(bf16[3024,384]{1,0:T(8,128)(2,1)S(1)} %copy-done.12, bf16[3024,1536]{1,0:T(8,128)(2,1)} %get-tuple-element.180), kind=kOutput, calls=%fused_computation.354 | convolution fusion | flops 3567255552 | bytes 13971456 | tf_op jit(solution)/shard_map/dot_general | solution.py:123
  297.4 15.0 %dot_general.23 = bf16[42,12,6,1536]{3,2,1,0:T(8,128)(2,1)} reshape(bf16[3024,1536]{1,0:T(8,128)(2,1)} %get-tuple-element.180) | data formatting | bytes 18579456 | tf_op jit(solution)/shard_map/dot_general | solution.py:126
  312.4 15.2 %multiply_reduce_fusion = (f32[384]{0:T(512)S(1)}, f32[42,12,6]{0,2,1:T(8,128)S(1)}, f32[42,12,6]{0,2,1:T(8,128)S(1)}, f32[384]{0:T(512)S(1)}, f32[42,12,6,384]{3,0,2,1:T(8,128)S(1)}) fusion(f32[42,12,6,384]{3,0,2,1:T(8,128)} %copy-done.4, f32[42,12,6]{0,2,1:T(8,128)S(1)} %copy-done.22, f32[42,12,6]{0,2,1:T(8,128)S(1)} %copy-done.20, ...), kind=kOutput, calls=%fused_computation.334 | convolution fusion | flops 3577699328 | bytes 19886720 | tf_op jit(solution)/shard_map/dot_general | solution.py:126
  327.7 7.1 %fusion.131 = (f32[384]{0:T(512)S(1)}, f32[384]{0:T(512)S(1)}, f32[384]{0:T(512)S(1)}, bf16[42,12,6,384]{3,0,2,1:T(8,128)(2,1)S(1)}) fusion(bf16[42,15,6,384]{3,0,2,1:T(8,128)(2,1)S(1)} %copy-done.3, f32[42,12,6]{0,2,1:T(8,128)S(1)} %get-tuple-element.181, f32[42,12,6,384]{3,0,2,1:T(8,128)} %copy-done.4, f32[42,12,6]{0,2,1:T(8,128)S(1)} %copy-done.20, ...), kind=kLoop, calls=%fused_computation.329 | loop fusion | flops 20900736 | bytes 18633984 | tf_op jit(solution)/shard_map/reduce_sum | solution.py:143
  334.9 7.7 %fusion.132 = (f32[384]{0:T(512)S(1)}, f32[384]{0:T(512)S(1)}, f32[384]{0:T(512)S(1)}, f32[384]{0:T(512)S(1)}, f32[384]{0:T(512)S(1)}, /*index=5*/f32[384]{0:T(5...) fusion(bf16[42,12,6,384]{3,0,2,1:T(8,128)(2,1)S(1)} %get-tuple-element., ...), kind=kLoop, calls=%fused_computation.330 | loop fusion | flops 44121984 | bytes 18596352 | tf_op jit(solution)/shard_map/reduce_sum | solution.py:143
  342.7 7.7 %fusion.129 = (f32[384]{0:T(512)S(1)}, f32[384]{0:T(512)S(1)}, f32[384]{0:T(512)S(1)}, f32[384]{0:T(512)S(1)}, f32[384]{0:T(512)S(1)}, /*index=5*/f32[384]{0:T(5...) fusion(bf16[42,12,6,384]{3,0,2,1:T(8,128)(2,1)S(1)} %get-tuple-element.151, ...), kind=kLoop, calls=%fused_computation.327 | loop fusion | flops 42961536 | bytes 7561728 | tf_op jit(solution)/shard_map/reduce_sum | solution.py:143
  350.5 7.8 %fusion.130 = (f32[384]{0:T(512)S(1)}, f32[384]{0:T(512)S(1)}, f32[384]{0:T(512)S(1)}, f32[384]{0:T(512)S(1)}, f32[384]{0:T(512)S(1)}, /*index=5*/f32[384]{0:T(5...) fusion(bf16[42,12,6,384]{3,0,2,1:T(8,128)(2,1)S(1)} %get-tuple-element.151, ...), kind=kLoop, calls=%fused_computation.328 | loop fusion | flops 42961536 | bytes 7561728 | tf_op jit(solution)/shard_map/reduce_sum | solution.py:143
  358.4 7.5 %fusion.133 = (f32[384]{0:T(512)S(1)}, f32[384]{0:T(512)S(1)}, f32[384]{0:T(512)S(1)}, f32[384]{0:T(512)S(1)}, f32[384]{0:T(512)S(1)}, /*index=5*/f32[384]{0:T(5...) fusion(bf16[42,12,6,384]{3,0,2,1:T(8,128)(2,1)S(1)} %get-tuple-element.151, ...), kind=kLoop, calls=%fused_computation.331 | loop fusion | flops 42961536 | bytes 7561728 | tf_op jit(solution)/shard_map/reduce_sum | solution.py:143
  365.9 7.6 %fusion.134 = (f32[384]{0:T(512)S(1)}, f32[384]{0:T(512)S(1)}, f32[384]{0:T(512)S(1)}, f32[384]{0:T(512)S(1)}, f32[384]{0:T(512)S(1)}, /*index=5*/f32[384]{0:T(5...) fusion(bf16[42,12,6,384]{3,0,2,1:T(8,128)(2,1)S(1)} %get-tuple-element.151, ...), kind=kLoop, calls=%fused_computation.332 | loop fusion | flops 42961536 | bytes 7561728 | tf_op jit(solution)/shard_map/reduce_sum | solution.py:143
  398.2 13.1 %all-reduce = f32[1536]{0:T(1024)S(1)} all-reduce(f32[1536]{0:T(1024)S(1)} %get-tuple-element.179), channel_id=4, replica_groups=mesh['ha'=2,'wa'=4,'ba'=4] {'ba'}, use_global_device_ids=true, to_apply=%region_64.65.clone | all-reduce | flops 1536 | bytes 12288
  412.3 89.7 %all-reduce.1 = (f32[54,96]{1,0:T(8,128)S(1)}, f32[384]{0:T(512)S(1)}) all-reduce(f32[54,96]{1,0:T(8,128)S(1)} %copy.53, f32[384]{0:T(512)S(1)} %dynamic-slice.1), channel_id=1, replica_groups=mesh['ha'=2,'wa'=4,'ba'=4] {'ha','wa'}, use_global_device_ids=true, to_apply=%region_60.61 | all-reduce | flops 5568 | bytes 44544 | tf_op jit(solution)/shard_map/psum | solution.py:154
  504.8 8.6 %pad_maximum_fusion = (bf16[42,18,9,384]{3,0,2,1:T(8,128)(2,1)}, bf16[42,18,9,384]{3,0,2,1:T(8,128)(2,1)}) fusion(bf16[42,18,3,384]{3,0,2,1:T(8,128)(2,1)} %collective-permute-done.6, bf16[42,3,6,384]{3,0,2,1:T(8,128)(2,1)S(1)} %collective-permute-done.5, bf16[42,12,6,384]{3,0,2,1:T(8,128)(2,1)S(1)} %get-tuple-element.151, ...), kind=kLoop, calls=%fused_computation.204 | loop fusion | flops 15676416 | bytes 17418240 | tf_op jit(solution)/shard_map/concatenate | solution.py:17
  513.9 49.3 %fusion.58 = bf16[42,12,6,384]{3,0,2,1:T(8,128)(2,1)} fusion(bf16[42,12,6,384]{3,0,2,1:T(8,128)(2,1)} %param.17, bf16[42,12,6,384]{3,0,2,1:T(8,128)(2,1)S(1)} %get-tuple-element.151, bf16[42,3,6,384]{3,0,2,1:T(8,128)(2,1)} %copy-done.14, bf16[42,3,6,384]{3,0,2,1:T(8,128)(2,1)S(1)} %collective-permute-done.5, ...), kind=kLoop, calls=%fused_computation.256 | loop fusion | flops 179988480 | bytes 105745920 | tf_op jit(solution)/shard_map/convert_element_type | solution.py:146
  563.2 8.8 %all-reduce.4.cloned.1.call-done = f32[2,384,384]{2,1,0:T(8,128)} async-done(((f32[2,384,384]{2,1,0:T(8,128)}), f32[2,384,384]{2,1,0:T(8,128)}) %all-reduce.4.cloned.1.call-update) | async-done | bytes 1179664 | tf_op jit(solution)/shard_map/psum | solution.py:154
  (361 shorter events, 83.7 us)
Async XLA Ops:
  7.2 175.0 %all-gather.4.cloned.1.call-start = ((), (), s32[]{:S(2)}) async-start(), calls=%async_computation.2 | async-start | bytes 2949120 | tf_op jit(solution)/shard_map/all_gather | solution.py:78
  8.8 4.1 collective-permute-start
  11.3 4.0 collective-permute-start.1
  19.8 47.8 %collective-permute-start.2 = (bf16[42,18,3,384]{3,0,2,1:T(8,128)(2,1)}, bf16[42,18,3,384]{3,0,2,1:T(8,128)(2,1)}, u32[]{:S(2)}, u32[]{:S(2)}) collective-permute-start(bf16[42,18,3,384]{3,0,2,1:T(8,128)(2,1)} %get-tuple-element.162), channel_id=1, source_target_pairs={{0,4},{4,8},{8,12},{1,5},{5,9},{9,13},{2,6},{6,10},{10,14},{3,7},{... | collective-permute-start | bytes 5225480 | tf_op jit(solution)/shard_map/ppermute | solution.py:19
  25.4 86.9 %collective-permute-start.3 = (bf16[42,18,3,384]{3,0,2,1:T(8,128)(2,1)}, bf16[42,18,3,384]{3,0,2,1:T(8,128)(2,1)}, u32[]{:S(2)}, u32[]{:S(2)}) collective-permute-start(bf16[42,18,3,384]{3,0,2,1:T(8,128)(2,1)} %get-tuple-element.163), channel_id=1, source_target_pairs={{4,0},{8,4},{12,8},{5,1},{9,5},{13,9},{6,2},{10,6},{14,10},{7,3},{... | collective-permute-start | bytes 5225480 | tf_op jit(solution)/shard_map/ppermute | solution.py:21
  27.6 383.8 %reduce-scatter.7.cloned.1.call-start = ((), (), s32[]{:S(2)}) async-start(), calls=%async_computation.5 | async-start | bytes 245760
  54.9 117.2 %copy-start.35 = (f32[384]{0:T(512)}, f32[384]{0:T(512)S(1)}, u32[]{:S(2)}) copy-start(f32[384]{0:T(512)S(1)} %get-tuple-element.120) | copy-start | bytes 4612
  54.9 117.2 %copy-start.37 = (f32[384]{0:T(512)}, f32[384]{0:T(512)S(1)}, u32[]{:S(2)}) copy-start(f32[384]{0:T(512)S(1)} %get-tuple-element.121) | copy-start | bytes 4612
  54.9 117.2 %copy-start.39 = (f32[384]{0:T(512)}, f32[384]{0:T(512)S(1)}, u32[]{:S(2)}) copy-start(f32[384]{0:T(512)S(1)} %get-tuple-element.122) | copy-start | bytes 4612
  55.0 117.2 %copy-start.41 = (f32[384]{0:T(512)}, f32[384]{0:T(512)S(1)}, u32[]{:S(2)}) copy-start(f32[384]{0:T(512)S(1)} %get-tuple-element.123) | copy-start | bytes 4612
  55.0 117.2 %copy-start.43 = (f32[384]{0:T(512)}, f32[384]{0:T(512)S(1)}, u32[]{:S(2)}) copy-start(f32[384]{0:T(512)S(1)} %get-tuple-element.124) | copy-start | bytes 4612
  55.0 117.2 %copy-start.45 = (f32[384]{0:T(512)}, f32[384]{0:T(512)S(1)}, u32[]{:S(2)}) copy-start(f32[384]{0:T(512)S(1)} %get-tuple-element.125) | copy-start | bytes 4612
  55.0 117.2 %copy-start.47 = (f32[384]{0:T(512)}, f32[384]{0:T(512)S(1)}, u32[]{:S(2)}) copy-start(f32[384]{0:T(512)S(1)} %get-tuple-element.126) | copy-start | bytes 4612
  55.0 117.2 %copy-start.49 = (f32[384]{0:T(512)}, f32[384]{0:T(512)S(1)}, u32[]{:S(2)}) copy-start(f32[384]{0:T(512)S(1)} %get-tuple-element.127) | copy-start | bytes 4612
  55.0 117.2 %copy-start.51 = (f32[384]{0:T(512)}, f32[384]{0:T(512)S(1)}, u32[]{:S(2)}) copy-start(f32[384]{0:T(512)S(1)} %get-tuple-element.128) | copy-start | bytes 4612
  55.0 117.2 %copy-start.53 = (f32[384]{0:T(512)}, f32[384]{0:T(512)S(1)}, u32[]{:S(2)}) copy-start(f32[384]{0:T(512)S(1)} %get-tuple-element.129) | copy-start | bytes 4612
  55.0 117.2 %copy-start.55 = (f32[384]{0:T(512)}, f32[384]{0:T(512)S(1)}, u32[]{:S(2)}) copy-start(f32[384]{0:T(512)S(1)} %get-tuple-element.130) | copy-start | bytes 4612
  56.1 117.7 %copy-start.31 = (f32[384]{0:T(512)}, f32[384]{0:T(512)S(1)}, u32[]{:S(2)}) copy-start(f32[384]{0:T(512)S(1)} %get-tuple-element.84) | copy-start | bytes 4612
  374.7 138.8 %reduce-scatter.5.cloned.1.call-start = ((), (), s32[]{:S(2)}) async-start(), calls=%async_computation.3 | async-start | bytes 5898240 | tf_op jit(solution)/shard_map/reduce_scatter | solution.py:156
  379.6 192.4 %all-reduce.4.cloned.1.call-start = ((), (), s32[]{:S(2)}) async-start(), calls=%async_computation.4 | async-start | bytes 2359296 | tf_op jit(solution)/shard_map/psum | solution.py:154
  379.8 4.4 collective-permute-start.5
  381.1 4.8 collective-permute-start.4
  389.8 114.9 %collective-permute-start.6 = (bf16[42,18,3,384]{3,0,2,1:T(8,128)(2,1)}, bf16[42,18,3,384]{3,0,2,1:T(8,128)(2,1)}, u32[]{:S(2)}, u32[]{:S(2)}) collective-permute-start(bf16[42,18,3,384]{3,0,2,1:T(8,128)(2,1)} %get-tuple-element.160), channel_id=1, source_target_pairs={{4,0},{8,4},{12,8},{5,1},{9,5},{13,9},{6,2},{10,6},{14,10},{7,3},{... | collective-permute-start | bytes 5225480 | tf_op jit(solution)/shard_map/ppermute | solution.py:21
  391.1 113.7 %collective-permute-start.7 = (bf16[42,18,3,384]{3,0,2,1:T(8,128)(2,1)}, bf16[42,18,3,384]{3,0,2,1:T(8,128)(2,1)}, u32[]{:S(2)}, u32[]{:S(2)}) collective-permute-start(bf16[42,18,3,384]{3,0,2,1:T(8,128)(2,1)} %get-tuple-element.161), channel_id=1, source_target_pairs={{0,4},{4,8},{8,12},{1,5},{5,9},{9,13},{2,6},{6,10},{10,14},{3,7},{... | collective-permute-start | bytes 5225480 | tf_op jit(solution)/shard_map/ppermute | solution.py:19
  (107 other events, 4772.2 us)
Sparse Core Ops, SparseCore 0:
  27.7 53.4 all-gather.3
  374.8 19.8 reduce-scatter.6
  397.1 83.9 reduce-scatter.4
  513.6 58.2 all-reduce.3
where the time goes:
time: 590 us; the launch traced here: 586 us
  other arithmetic  189 us (32%)
  blocking collectives  129 us (22%)
  matrix products  108 us (18%)
  waiting for transfers between devices  66.2 us (11%)
  local copies, waits for them, and re-layouts  54.4 us (9%)
  starting transfers between devices  22.3 us (4%)
  between operations  17.6 us (3%)
    psum x1, blocking collectives, local(): whole = lax.psum((mats_local, chan_local, grad_hbias), ('ha', 'wa'))  89.7 us
    reduce_sum x1, other arithmetic, local(): center = conv - jnp.mean(conv, axis=-1, keepdims=True)  59.9 us
    convert_element_type x1, other arithmetic, local(): (upstream + depthwise(grad_padded, taps, tile_rows, tile_cols, True)).ast...  49.3 us
    dot_general x1, matrix products, local(): jnp.dot(flat_in, w_in, preferred_element_type=jnp.float32) + hid_bias  46 us
    ppermute x4, waiting for transfers between devices, with_halo(): lax.ppermute(head, axis, [((i + 1) % count, i) for i in range(ends)])  45.6 us
    reduce_sum x6, other arithmetic, local(): jnp.sum(piece * conv_grad.astype(jnp.float32), axis=(0, 1, 2))  45.3 us
    dot_general x1, matrix products, local(): act_grad = jnp.dot(flat_branch, w_out, preferred_element_type=jnp.float32)  22.9 us
    ppermute x4, starting transfers between devices, with_halo(): lax.ppermute(tail, axis, [(i, (i + 1) % count) for i in range(ends)])  16.9 us
  transfers between devices with their start and end apart: 12, of which 6 were waited for; matrix products, arithmetic and copies ran while one was open for 24% of the time, Pallas kernels for 0%

commit v1 on v0

v1 whole, which is shorter than its diff:
```python
import functools
import jax
import jax.numpy as jnp
from jax import lax
from jax.experimental import pallas as pl
from jax.experimental.pallas import tpu as pltpu
from jax.sharding import PartitionSpec as P

STEP = 3
C=384; HID=1536; KS=7; R=3
F32=jnp.float32; BF=jnp.bfloat16

def conv_pair(xf, k_ref, cb_ref, z_ref, h, zr, N, TW):
    def step(t, _):
        ct = t // (N//8); nt = t % (N//8)
        c = pl.ds(pl.multiple_of(ct*128,128),128); n = pl.ds(pl.multiple_of(nt*8,8),8)
        b = jnp.broadcast_to(cb_ref[0:1, c],(8,128))
        acc=[[b]*TW for _ in range(2)]
        for ii in range(KS+1):
            row=[xf[h+ii, w, n, c] for w in range(TW+KS-1)]
            for r in range(2):
                i=ii-r
                if 0<=i<KS:
                    for j in range(KS):
                        kk=k_ref[i*KS+j, pl.ds(0,1), c]
                        for w in range(TW):
                            acc[r][w]=acc[r][w]+row[w+j]*kk
        for r in range(2):
            for w in range(TW):
                z_ref[zr+r, w, n, c]=acc[r][w]
        return 0
    lax.fori_loop(0, 3*(N//8), step, 0)

def widen(x_ref, xf, rows, cols):
    def step(t,_):
        for w in range(cols):
            xf[t, w]=x_ref[t, w].astype(F32)
        return 0
    lax.fori_loop(0, rows, step, 0)

def conv_fwd(xpad, taps, cb):
    HP,WP,N,_=xpad.shape; TH,TW=HP-6,WP-6
    def body(x_ref,k_ref,cb_ref,z_ref,xf):
        g=pl.program_id(0)
        @pl.when(g==0)
        def _(): widen(x_ref,xf,HP,WP)
        conv_pair(xf,k_ref,cb_ref,z_ref,2*g,0,N,TW)
    return pl.pallas_call(body,out_shape=jax.ShapeDtypeStruct((TH,TW,N,C),F32),grid=(TH//2,),
        in_specs=[pl.BlockSpec((HP,WP,N,C),lambda g:(0,0,0,0),pipeline_mode=pl.Buffered(1)),
                  pl.BlockSpec((49,1,C),lambda g:(0,0,0)),pl.BlockSpec((1,C),lambda g:(0,0))],
        out_specs=pl.BlockSpec((2,TW,N,C),lambda g:(g,0,0,0)),
        scratch_shapes=[pltpu.VMEM((HP,WP,N,C),F32)],
        compiler_params=pltpu.CompilerParams(vmem_limit_bytes=60<<20),name="conv_fwd")(xpad,taps.reshape(49,1,C),cb)

def conv_back_row(df, k_ref, x_ref, og_ref, ig_ref, gk, h, hr, N, TW):
    def step(t, _):
        ct = t // (N//8); nt = t % (N//8)
        c = pl.ds(pl.multiple_of(ct*128,128),128); n = pl.ds(pl.multiple_of(nt*8,8),8)
        x=[x_ref[hr, w, n, c].astype(F32) for w in range(TW)]
        acc=[og_ref[hr, w, n, c].astype(F32) for w in range(TW)]
        for i in range(KS):
            row=[df[h+6-i, w, n, c] for w in range(TW+KS-1)]
            for j in range(KS):
                kk=k_ref[i*KS+j, pl.ds(0,1), c]
                s=None
                for w in range(TW):
                    d=row[w+6-j]
                    acc[w]=acc[w]+d*kk
                    p=d*x[w]
                    s=p if s is None else s+p
                gk[i*KS+j,:,c]=gk[i*KS+j,:,c]+s
        for w in range(TW):
            ig_ref[hr, w, n, c]=acc[w].astype(BF)
        return 0
    lax.fori_loop(0, 3*(N//8), step, 0)

def conv_back(dzpad, x, og, taps):
    HP,WP,N,_=dzpad.shape; TH,TW=HP-6,WP-6
    def body(d_ref,k_ref,x_ref,og_ref,ig_ref,gk_ref,df,gk):
        g=pl.program_id(0)
        @pl.when(g==0)
        def _():
            widen(d_ref,df,HP,WP)
            gk[...]=jnp.zeros_like(gk)
        conv_back_row(df,k_ref,x_ref,og_ref,ig_ref,gk,g,0,N,TW)
        @pl.when(g==pl.num_programs(0)-1)
        def _(): gk_ref[...]=jnp.sum(gk[...],axis=1)
    return pl.pallas_call(body,out_shape=(jax.ShapeDtypeStruct((TH,TW,N,C),BF),jax.ShapeDtypeStruct((49,C),F32)),grid=(TH,),
        in_specs=[pl.BlockSpec((HP,WP,N,C),lambda g:(0,0,0,0),pipeline_mode=pl.Buffered(1)),
                  pl.BlockSpec((49,1,C),lambda g:(0,0,0)),
                  pl.BlockSpec((1,TW,N,C),lambda g:(g,0,0,0)),pl.BlockSpec((1,TW,N,C),lambda g:(g,0,0,0))],
        out_specs=(pl.BlockSpec((1,TW,N,C),lambda g:(g,0,0,0)),pl.BlockSpec((49,C),lambda g:(0,0))),
        scratch_shapes=[pltpu.VMEM((HP,WP,N,C),F32),pltpu.VMEM((49,8,C),F32)],
        compiler_params=pltpu.CompilerParams(vmem_limit_bytes=60<<20),name="conv_back")(dzpad,taps.reshape(49,1,C),x,og)

P0=0.3275911; A1=0.254829592; A2=-0.284496736; A3=1.421413741; A4=-1.453152027; A5=1.061405429
def gelu_pair(v):
    s=0.7071067811865476
    a=jnp.abs(v)
    t=1.0/(1.0+(P0*s)*a)
    e=jnp.exp(v*v*-0.5)
    q=t*(0.5*A1+t*(0.5*A2+t*(0.5*A3+t*(0.5*A4+t*(0.5*A5)))))*e
    phi=jnp.where(v>0,1.0-q,q)
    return v*phi, phi+v*e*0.3989422804014327

def dg(a,b,ca,cb): return lax.dot_general(a,b,(((ca,),(cb,)),((),())),preferred_element_type=F32)

def mlp_block(z, og, xc, gate, wi, wo, bi_ref, ch_ref, outs, acc, HC):
    gain=ch_ref[1:2]; shift=ch_ref[2:3]; bo=ch_ref[3:4]; ls=ch_ref[4:5]
    out_ref,dz_ref=outs; gwi,gwo,gch,gbi=acc
    mu=jnp.mean(z,axis=1,keepdims=True)
    zc=z-mu
    inv=lax.rsqrt(jnp.mean(zc*zc,axis=1,keepdims=True)+1e-6)
    xhat=zc*inv
    xn=(xhat*gain+shift).astype(BF)
    gog=gate*og.astype(F32)
    db=(gog*ls).astype(BF)
    M=z.shape[0]
    branch=jnp.zeros((M,C),F32); dxn=jnp.zeros((M,C),F32)
    for j in range(HID//HC):
        hs=slice(j*HC,(j+1)*HC)
        pre=dg(xn,wi[:,hs],1,0)+bi_ref[0:1,hs]
        da=dg(db,wo[:,hs],1,0)
        act,gp=gelu_pair(pre)
        act=act.astype(BF)
        dpre32=da*gp
        dpre=dpre32.astype(BF)
        branch+=dg(act,wo[:,hs],1,1)
        dxn+=dg(dpre,wi[:,hs],1,1)
        gwo[:,hs]+=dg(db,act,0,0)
        gwi[:,hs]+=dg(xn,dpre,0,0)
        gbi[:,hs]+=jnp.sum(dpre.astype(F32).reshape(M//8,8,HC),axis=0)
    branch+=bo
    out_ref[...]=(xc.astype(F32)+gate*ls*branch).astype(BF)
    q=dxn*gain
    m1=jnp.mean(q,axis=1,keepdims=True); m2=jnp.mean(q*xhat,axis=1,keepdims=True)
    dz=(inv*(q-m1-xhat*m2)).astype(BF)
    dz_ref[...]=dz
    red=lambda v: jnp.sum(v.reshape(M//8,8,C),axis=0)
    gch[0]+=red(dz.astype(F32)); gch[1]+=red(dxn*xhat); gch[2]+=red(dxn)
    gch[3]+=red(db.astype(F32)); gch[4]+=red(gog*branch)

def mlp(z, og, xc, gate, wi, wo, bi, ch, steps=6, HC=512):
    rows=z.shape[0]; M=rows//steps
    def body(z_ref,og_ref,xc_ref,g_ref,wi_ref,wo_ref,bi_ref,ch_ref,out_ref,dz_ref,gwi_ref,gwo_ref,gch_ref,gbi_ref,gch,gbi):
        s=pl.program_id(0)
        @pl.when(s==0)
        def _():
            gwi_ref[...]=jnp.zeros_like(gwi_ref); gwo_ref[...]=jnp.zeros_like(gwo_ref)
            gch[...]=jnp.zeros_like(gch); gbi[...]=jnp.zeros_like(gbi)
        mlp_block(z_ref[...],og_ref[...],xc_ref[...],g_ref[:,0:1],wi_ref,wo_ref,bi_ref,ch_ref,(out_ref,dz_ref),(gwi_ref,gwo_ref,gch,gbi),HC)
        @pl.when(s==steps-1)
        def _():
            gch_ref[...]=jnp.sum(gch[...],axis=1); gbi_ref[...]=jnp.sum(gbi[...],axis=0,keepdims=True)
    full=lambda *sh: pl.BlockSpec(sh,lambda s:(0,)*len(sh))
    blk=pl.BlockSpec((M,C),lambda s:(s,0))
    return pl.pallas_call(body,out_shape=(jax.ShapeDtypeStruct((rows,C),BF),jax.ShapeDtypeStruct((rows,C),BF),
            jax.ShapeDtypeStruct((C,HID),F32),jax.ShapeDtypeStruct((C,HID),F32),jax.ShapeDtypeStruct((8,C),F32),jax.ShapeDtypeStruct((1,HID),F32)),
        grid=(steps,),in_specs=[blk,blk,blk,full(M,128),full(C,HID),full(C,HID),full(1,HID),full(8,C)],
        out_specs=(blk,blk,full(C,HID),full(C,HID),full(8,C),full(1,HID)),
        scratch_shapes=[pltpu.VMEM((8,8,C),F32),pltpu.VMEM((8,HID),F32)],
        compiler_params=pltpu.CompilerParams(vmem_limit_bytes=62<<20),name="mlp")(z,og,xc,gate,wi,wo,bi,ch)


def with_halo(cells, sides, width):
    for axis, dim in sides:
        count = lax.axis_size(axis)
        ends = count - 1
        head = lax.slice_in_dim(cells, 0, width, axis=dim)
        tail = lax.slice_in_dim(cells, cells.shape[dim] - width, cells.shape[dim], axis=dim)
        cells = jnp.concatenate(
            [
                lax.ppermute(tail, axis, [(i, (i + 1) % count) for i in range(ends)]),
                cells,
                lax.ppermute(head, axis, [((i + 1) % count, i) for i in range(ends)]),
            ],
            axis=dim,
        )
    return cells


def adam_step(master, grad, moment, second, average, rate):
    moment_new = 0.5 * moment + 0.5 * grad
    second_new = 0.5 * second + 0.5 * grad * grad
    correct = 1.0 - 0.5**STEP
    master_new = master - rate * (
        moment_new / correct / (jnp.sqrt(second_new / correct) + 1e-08) + 0.05 * master
    )
    average_new = 0.9 * average + 0.1 * master_new
    return (master_new, moment_new, second_new, average_new)


def local(
    images,
    out_grad,
    keep_mask,
    img_counts,
    mats_master,
    chan_master,
    bias_master,
    mats_moment,
    chan_moment,
    bias_moment,
    mats_second,
    chan_second,
    bias_second,
    mats_average,
    chan_average,
    bias_average,
):
    n_img, rows, cols = images.shape[0], images.shape[1], images.shape[2]
    slots = -(-n_img // 16) * 16
    mats_all, chan_all, bias_all = (
        lax.all_gather(mats_master.astype(BF), "ba", axis=2, tiled=True),
        lax.all_gather(chan_master.astype(BF), "ba", axis=1, tiled=True),
        lax.all_gather(bias_master.astype(BF), "ba", axis=0, tiled=True),
    )
    chan_vals = chan_all.astype(F32)
    taps, rest = chan_vals[:49], jnp.pad(chan_vals[49:], ((0, 3), (0, 0)))
    fill = jnp.arange(n_img, dtype=jnp.int32) < img_counts[0]
    gate = jnp.pad(jnp.where(fill, keep_mask, 0).astype(F32), (0, slots - n_img))
    steps = rows // 2
    gate = jnp.broadcast_to(jnp.tile(gate, 2 * cols)[:, None], (2 * cols * slots, 128))
    pad = ((0, 0), (0, 0), (0, slots - n_img), (0, 0))
    x = jnp.pad(images.transpose(1, 2, 0, 3), pad)
    up = jnp.pad(out_grad.transpose(1, 2, 0, 3), pad)
    halo = (("ha", 0), ("wa", 1))
    z = conv_fwd(with_halo(x, halo, R), taps, rest[:1])
    flat = lambda v: v.reshape(-1, C)
    out, dz, grad_win, grad_wout, gch, gbi = mlp(
        flat(z), flat(up), flat(x), gate, mats_all[0], mats_all[1], bias_all.astype(F32)[None], rest, steps
    )
    dzp = with_halo(dz.reshape(rows, cols, slots, C), halo, R)
    ig, grad_taps = conv_back(dzp, x, up, taps)
    back = lambda v: v.reshape(rows, cols, slots, C)[:, :, :n_img].transpose(2, 0, 1, 3)
    outputs, input_grad = back(out), back(ig)
    mats_local = jnp.stack([grad_win, grad_wout], axis=0)
    chan_local = jnp.concatenate([grad_taps, gch[:5]], axis=0)
    grad_hbias = gbi[0]
    whole = lax.psum((mats_local, chan_local, grad_hbias), ("ha", "wa"))
    mats_grad, chan_grad, bias_grad = (
        lax.psum_scatter(whole[0], "ba", scatter_dimension=2, tiled=True),
        lax.psum_scatter(whole[1], "ba", scatter_dimension=1, tiled=True),
        lax.psum_scatter(whole[2], "ba", scatter_dimension=0, tiled=True),
    )
    mats_new, mats_moment_new, mats_second_new, mats_average_new = adam_step(
        mats_master, mats_grad, mats_moment, mats_second, mats_average, 0.03
    )
    chan_new, chan_moment_new, chan_second_new, chan_average_new = adam_step(
        chan_master, chan_grad, chan_moment, chan_second, chan_average, 0.3
    )
    bias_new, bias_moment_new, bias_second_new, bias_average_new = adam_step(
        bias_master, bias_grad, bias_moment, bias_second, bias_average, 0.3
    )
    return (
        outputs,
        input_grad,
        mats_grad,
        chan_grad,
        bias_grad,
        mats_new,
        chan_new,
        bias_new,
        mats_moment_new,
        chan_moment_new,
        bias_moment_new,
        mats_second_new,
        chan_second_new,
        bias_second_new,
        mats_average_new,
        chan_average_new,
        bias_average_new,
        mats_new.astype(jnp.bfloat16),
        chan_new.astype(jnp.bfloat16),
        bias_new.astype(jnp.bfloat16),
    )


def solution(mesh):
    return jax.shard_map(
        local,
        mesh=mesh,
        in_specs=(
            P("ba", "ha", "wa", None),
            P("ba", "ha", "wa", None),
            P("ba"),
            P("ba"),
            P(None, None, "ba"),
            P(None, "ba"),
            P("ba"),
            P(None, None, "ba"),
            P(None, "ba"),
            P("ba"),
            P(None, None, "ba"),
            P(None, "ba"),
            P("ba"),
            P(None, None, "ba"),
            P(None, "ba"),
            P("ba"),
        ),
        out_specs=(
            P("ba", "ha", "wa", None),
            P("ba", "ha", "wa", None),
            P(None, None, "ba"),
            P(None, "ba"),
            P("ba"),
            P(None, None, "ba"),
            P(None, "ba"),
            P("ba"),
            P(None, None, "ba"),
            P(None, "ba"),
            P("ba"),
            P(None, None, "ba"),
            P(None, "ba"),
            P("ba"),
            P(None, None, "ba"),
            P(None, "ba"),
            P("ba"),
            P(None, None, "ba"),
            P(None, "ba"),
            P("ba"),
        ),
        check_vma=False,
    )
```

time: 590 us -> 539 us (0.914)
  waiting for transfers between devices: 66.2 us -> 251 us
  other arithmetic: 189 us -> 29.5 us
  Pallas kernels: 0 us -> 129 us
  matrix products: 108 us -> 0 us
  blocking collectives: 129 us -> 64.1 us
  local copies, waits for them, and re-layouts: 54.4 us -> 28.6 us
    pallas_call x0 -> x3, Pallas kernels: none -> 129 us  [the longest x1 55.7 us: mlp(): pl.pallas_call(body, out_shape=(jax.ShapeDtypeStruct((rows, C), BF), jax....]
    reduce_sum x9 -> x0, other arithmetic: 113 us -> none  [the longest x1 59.9 us: local(): center = conv - jnp.mean(conv, axis=-1, keepdims=True)]
    dot_general x6 -> x0, matrix products: 108 us -> none  [the longest x1 46 us: local(): jnp.dot(flat_in, w_in, preferred_element_type=jnp.float32) + hid_bias]
    psum x1, blocking collectives: 89.7 us -> 24.6 us  [local(): whole = lax.psum((mats_local, chan_local, grad_hbias), ('ha', 'wa'))]
    reduce_scatter x1, waiting for transfers between devices: 0.02 us -> 55 us  [local(): lax.psum_scatter(whole[0], 'ba', scatter_dimension=2, tiled=True)]
    convert_element_type x6 -> x3, other arithmetic: 51.9 us -> 0.89 us  [the longest x1 0.88 us: local(): mats_master.astype(BF)]
    psum x1, waiting for transfers between devices: 8.79 us -> 59 us  [local(): whole = lax.psum((mats_local, chan_local, grad_hbias), ('ha', 'wa'))]
    ppermute x4, waiting for transfers between devices: 45.6 us -> 88 us  [with_halo(): lax.ppermute(head, axis, [((i + 1) % count, i) for i in range(ends)])]
  transfers between devices with their start and end apart: 12 -> 12, of which waited for: 6 -> 7; matrix products, arithmetic and copies ran while one was open for 24% -> 6% of each run, Pallas kernels for 0% -> 5%
where the time goes in v1:
time: 539 us; the launch traced here: 538 us
  waiting for transfers between devices  251 us (47%)
  Pallas kernels  129 us (24%)
  blocking collectives  64.1 us (12%)
  other arithmetic  29.5 us (5%)
  local copies, waits for them, and re-layouts  28.6 us (5%)
  starting transfers between devices  20.1 us (4%)
  between operations  15.5 us (3%)
    ppermute x4, waiting for transfers between devices, with_halo(): lax.ppermute(head, axis, [((i + 1) % count, i) for i in range(ends)])  88 us
    psum x1, waiting for transfers between devices, local(): whole = lax.psum((mats_local, chan_local, grad_hbias), ('ha', 'wa'))  59 us
    pallas_call x1, Pallas kernels, mlp(): pl.pallas_call(body, out_shape=(jax.ShapeDtypeStruct((rows, C), BF), jax....  55.7 us
    reduce_scatter x1, waiting for transfers between devices, local(): lax.psum_scatter(whole[0], 'ba', scatter_dimension=2, tiled=True)  55 us
    ppermute x4, waiting for transfers between devices, with_halo(): lax.ppermute(tail, axis, [(i, (i + 1) % count) for i in range(ends)])  49.5 us
    pallas_call x1, Pallas kernels, conv_back(): pl.pallas_call(body, out_shape=(jax.ShapeDtypeStruct((TH, TW, N, C), BF),...  44 us
    pallas_call x1, Pallas kernels, conv_fwd(): pl.pallas_call(body, out_shape=jax.ShapeDtypeStruct((TH, TW, N, C), F32),...  29 us
    psum x1, blocking collectives, local(): whole = lax.psum((mats_local, chan_local, grad_hbias), ('ha', 'wa'))  24.6 us
  transfers between devices with their start and end apart: 12, of which 7 were waited for; matrix products, arithmetic and copies ran while one was open for 6% of the time, Pallas kernels for 5%

profile of v1, /device:TPU:0, one launch (start us, length us, event | category | flops | bytes accessed | tf_op | source)
XLA Modules:
  0.0 537.9 jit_solution(16186962216807295798)
XLA Ops:
  7.2 2.6 pad_slice_fusion.1
  20.8 5.5 %collective-permute-start.2 = (bf16[18,3,48,384]{3,2,1,0:T(8,128)(2,1)}, bf16[18,3,48,384]{3,2,1,0:T(8,128)(2,1)}, u32[]{:S(2)}, u32[]{:S(2)}) collective-permute-start(bf16[18,3,48,384]{3,2,1,0:T(8,128)(2,1)} %get-tuple-element.52), channel_id=1, source_target_pairs={{0,4},{4,8},{8,12},{1,5},{5,9},{9,13},{2,6},{6,10},{10,14},{3,7},{... | collective-permute-start | bytes 5971976 | tf_op jit(solution)/shard_map/ppermute | solution.py:173
  27.6 14.9 %all-gather = bf16[4,96,54]{1,2,0:T(8,128)(2,1)S(1)} all-gather(bf16[1,96,54]{1,2,0:T(8,128)(2,1)S(1)} %convert_bitcast_fusion), channel_id=1, replica_groups=mesh['ha'=2,'wa'=4,'ba'=4] {'ba'}, dimensions={0}, use_global_device_ids=true | all-gather | bytes 51840 | tf_op jit(solution)/shard_map/all_gather | solution.py:215
  43.9 12.4 %all-gather.1 = bf16[4,1,384]{2,1,0:T(2,128)(2,1)S(1)} all-gather(bf16[1,1,384]{2,1,0:T(2,128)(2,1)S(1)} %reshape.72), channel_id=1, replica_groups=mesh['ha'=2,'wa'=4,'ba'=4] {'ba'}, dimensions={0}, use_global_device_ids=true | all-gather | bytes 3840 | tf_op jit(solution)/shard_map/all_gather | solution.py:216
  58.2 3.5 pad.16.og_ref
  61.8 6.3 %collective-permute-done.2 = bf16[18,3,48,384]{3,2,1,0:T(8,128)(2,1)} collective-permute-done((bf16[18,3,48,384]{3,2,1,0:T(8,128)(2,1)}, bf16[18,3,48,384]{3,2,1,0:T(8,128)(2,1)}, u32[]{:S(2)}, u32[]{:S(2)}) %collective-permute-start.2) | collective-permute-done | bytes 1990688 | tf_op jit(solution)/shard_map/ppermute | solution.py:173
  68.0 44.6 %collective-permute-done.3 = bf16[18,3,48,384]{3,2,1,0:T(8,128)(2,1)} collective-permute-done((bf16[18,3,48,384]{3,2,1,0:T(8,128)(2,1)}, bf16[18,3,48,384]{3,2,1,0:T(8,128)(2,1)}, u32[]{:S(2)}, u32[]{:S(2)}) %collective-permute-start.3) | collective-permute-done | bytes 1990688 | tf_op jit(solution)/shard_map/ppermute | solution.py:175
  112.7 7.3 %pad_maximum_fusion.x_ref = bf16[18,12,48,384]{3,2,1,0:T(8,128)(2,1)} fusion(bf16[18,3,48,384]{3,2,1,0:T(8,128)(2,1)} %collective-permute-done.3, bf16[3,6,48,384]{3,2,1,0:T(8,128)(2,1)} %collective-permute-done.1, bf16[12,6,48,384]{3,2,1,0:T(8,128)(2,1)S(1)} %pad.15.x_ref, bf16[3,6,48,384]{3,2,1,0:T(8,128)(2,1)S(1)} %collective-permute-done, ...), kind=kLoop, calls=%fused_computation | loop fusion | flops 15925248 | bytes 15925248 | tf_op jit(solution)/shard_map/concatenate | solution.py:171
  120.0 29.0 %conv_fwd.1 = f32[12,6,48,384]{3,2,1,0:T(8,128)} custom-call(bf16[18,12,48,384]{3,2,1,0:T(8,128)(2,1)} %pad_maximum_fusion.x_ref, f32[49,1,384]{2,1,0:T(1,128)} %reshape.63.k_ref, f32[1,384]{1,0:T(1,128)} %slice.77.cb_ref), custom_call_target="tpu_custom_call" | custom-call | tf_op jit(solution)/shard_map/conv_fwd/pallas_call | solution.py:48
  149.0 3.2 slice_bitcast_fusion.2
  153.0 55.7 %mlp.1 = (bf16[3456,384]{1,0:T(8,128)(2,1)}, bf16[3456,384]{1,0:T(8,128)(2,1)}, f32[384,1536]{1,0:T(8,128)}, f32[384,1536]{1,0:T(8,128)}, f32[8,384]{1,0:T(8,128)}, /*index=5*/f32[1,1536]{1,0:T(1,128)}) custom-call(f32[3456,384]{1,0:T(8,128)} %bitcast.37, bf16[3456,384]{1,0:T(8,128)(2,1)} %bitcast.36, bf16[3456,384]{1,0:T(8,128)(2,1)} %bitcast.35, ...), custom_call_target="tpu_custom_call" | custom-call | tf_op jit(solution)/shard_map/mlp/pallas_call | solution.py:157
  211.6 3.1 collective-permute-start.4
  217.4 3.5 collective-permute-start.6
  222.4 41.5 %collective-permute-done.6 = bf16[18,3,48,384]{3,2,1,0:T(8,128)(2,1)S(1)} collective-permute-done((bf16[18,3,48,384]{3,2,1,0:T(8,128)(2,1)S(1)}, bf16[18,3,48,384]{3,2,1,0:T(8,128)(2,1)S(1)}, u32[]{:S(2)}, u32[]{:S(2)}) %collective-permute-start.6) | collective-permute-done | bytes 1990688 | tf_op jit(solution)/shard_map/ppermute | solution.py:173
  263.9 43.4 %collective-permute-done.7 = bf16[18,3,48,384]{3,2,1,0:T(8,128)(2,1)S(1)} collective-permute-done((bf16[18,3,48,384]{3,2,1,0:T(8,128)(2,1)S(1)}, bf16[18,3,48,384]{3,2,1,0:T(8,128)(2,1)S(1)}, u32[]{:S(2)}, u32[]{:S(2)}) %collective-permute-start.7) | collective-permute-done | bytes 1990688 | tf_op jit(solution)/shard_map/ppermute | solution.py:175
  307.3 5.1 pad_maximum_fusion.1.d_ref
  312.4 44.0 %conv_back.1 = (bf16[12,6,48,384]{3,2,1,0:T(8,128)(2,1)}, f32[49,384]{1,0:T(8,128)}) custom-call(bf16[18,12,48,384]{3,2,1,0:T(8,128)(2,1)} %pad_maximum_fusion.1.d_ref, f32[49,1,384]{2,1,0:T(1,128)} %reshape.63.k_ref, bf16[12,6,48,384]{3,2,1,0:T(8,128)(2,1)} %copy-done, bf16[12,6,48,384]{3,2,1,0:T(8,128)(2,1)} %pad.16.og_ref), custom_call_target="tpu_custom_call" | custom-call | tf_op jit(solution)/shard_map/conv_back/pallas_call | solution.py:88
  358.2 4.4 pad_maximum_fusion.2
  364.6 12.2 %all-reduce.4 = f32[1536]{0:T(1024)S(1)} all-reduce(f32[1536]{0:T(1024)S(1)} %reduce), channel_id=4, replica_groups=mesh['ha'=2,'wa'=4,'ba'=4] {'ba'}, use_global_device_ids=true, to_apply=%region_5.6.clone | all-reduce | flops 1536 | bytes 12288
  377.0 5.0 slice_bitcast_fusion
  383.0 24.6 %all-reduce.5 = (f32[54,96]{1,0:T(8,128)S(1)}, f32[384]{0:T(512)S(1)}) all-reduce(f32[54,96]{1,0:T(8,128)S(1)} %copy.39, f32[384]{0:T(512)S(1)} %dynamic-slice.1), channel_id=1, replica_groups=mesh['ha'=2,'wa'=4,'ba'=4] {'ha','wa'}, use_global_device_ids=true, to_apply=%region_2.3 | all-reduce | flops 5568 | bytes 44544 | tf_op jit(solution)/shard_map/psum | solution.py:240
  408.2 55.0 %reduce-scatter.5.cloned.1.call-done = f32[2,384,384]{2,1,0:T(8,128)} async-done(((f32[2,384,1536]{2,1,0:T(8,128)}), f32[2,384,384]{2,1,0:T(8,128)}) %reduce-scatter.5.cloned.1.call-update) | async-done | bytes 1179664 | tf_op jit(solution)/shard_map/reduce_scatter | solution.py:242
  465.0 59.0 %all-reduce.8.cloned.1.call-done = f32[2,384,384]{2,1,0:T(8,128)} async-done(((f32[2,384,384]{2,1,0:T(8,128)}), f32[2,384,384]{2,1,0:T(8,128)}) %all-reduce.8.cloned.1.call-update) | async-done | bytes 1179664 | tf_op jit(solution)/shard_map/psum | solution.py:240
  524.0 4.2 fusion.8
  (103 shorter events, 32.5 us)
Async XLA Ops:
  7.2 141.8 %all-gather.4.cloned.1.call-start = ((), (), s32[]{:S(2)}) async-start(), calls=%async_computation.2 | async-start | bytes 2949120 | tf_op jit(solution)/shard_map/all_gather | solution.py:214
  9.8 6.8 %collective-permute-start = (bf16[3,6,48,384]{3,2,1,0:T(8,128)(2,1)}, bf16[3,6,48,384]{3,2,1,0:T(8,128)(2,1)S(1)}, u32[]{:S(2)}, u32[]{:S(2)}) collective-permute-start(bf16[3,6,48,384]{3,2,1,0:T(8,128)(2,1)} %get-tuple-element.56), channel_id=1, source_target_pairs={{0,16},{1,17},{2,18},{3,19},{4,20},{5,21},{6,22},{7,23},{8,24},{9,... | collective-permute-start | bytes 1990664 | tf_op jit(solution)/shard_map/ppermute | solution.py:173
  12.3 4.3 collective-permute-start.1
  14.5 367.5 %reduce-scatter.7.cloned.1.call-start = ((), (), s32[]{:S(2)}) async-start(), calls=%async_computation.5 | async-start | bytes 245760
  16.6 96.1 %copy-start = (bf16[12,6,48,384]{3,2,1,0:T(8,128)(2,1)}, bf16[12,6,48,384]{3,2,1,0:T(8,128)(2,1)S(1)}, u32[]{:S(2)}) copy-start(bf16[12,6,48,384]{3,2,1,0:T(8,128)(2,1)S(1)} %pad.15.x_ref) | copy-start | bytes 7962628
  20.8 47.2 %collective-permute-start.2 = (bf16[18,3,48,384]{3,2,1,0:T(8,128)(2,1)}, bf16[18,3,48,384]{3,2,1,0:T(8,128)(2,1)}, u32[]{:S(2)}, u32[]{:S(2)}) collective-permute-start(bf16[18,3,48,384]{3,2,1,0:T(8,128)(2,1)} %get-tuple-element.52), channel_id=1, source_target_pairs={{0,4},{4,8},{8,12},{1,5},{5,9},{9,13},{2,6},{6,10},{10,14},{3,7},{... | collective-permute-start | bytes 5971976 | tf_op jit(solution)/shard_map/ppermute | solution.py:173
  26.3 86.3 %collective-permute-start.3 = (bf16[18,3,48,384]{3,2,1,0:T(8,128)(2,1)}, bf16[18,3,48,384]{3,2,1,0:T(8,128)(2,1)}, u32[]{:S(2)}, u32[]{:S(2)}) collective-permute-start(bf16[18,3,48,384]{3,2,1,0:T(8,128)(2,1)} %get-tuple-element.53), channel_id=1, source_target_pairs={{4,0},{8,4},{12,8},{5,1},{9,5},{13,9},{6,2},{10,6},{14,10},{7,3},{... | collective-permute-start | bytes 5971976 | tf_op jit(solution)/shard_map/ppermute | solution.py:175
  210.3 4.4 collective-permute-start.5
  211.6 4.8 collective-permute-start.4
  217.4 46.5 %collective-permute-start.6 = (bf16[18,3,48,384]{3,2,1,0:T(8,128)(2,1)S(1)}, bf16[18,3,48,384]{3,2,1,0:T(8,128)(2,1)S(1)}, u32[]{:S(2)}, u32[]{:S(2)}) collective-permute-start(bf16[18,3,48,384]{3,2,1,0:T(8,128)(2,1)S(1)} %get-tuple-element.50), channel_id=1, source_target_pairs={{0,4},{4,8},{8,12},{1,5},{5,9},{9,13},{2,6},{6,10},{10,14},{3,7},{... | collective-permute-start | bytes 5971976 | tf_op jit(solution)/shard_map/ppermute | solution.py:173
  220.9 86.4 %collective-permute-start.7 = (bf16[18,3,48,384]{3,2,1,0:T(8,128)(2,1)S(1)}, bf16[18,3,48,384]{3,2,1,0:T(8,128)(2,1)S(1)}, u32[]{:S(2)}, u32[]{:S(2)}) collective-permute-start(bf16[18,3,48,384]{3,2,1,0:T(8,128)(2,1)S(1)} %get-tuple-element.51), channel_id=1, source_target_pairs={{4,0},{8,4},{12,8},{5,1},{9,5},{13,9},{6,2},{10,6},{14,10},{7,3},{... | collective-permute-start | bytes 5971976 | tf_op jit(solution)/shard_map/ppermute | solution.py:175
  312.4 45.8 %copy-start.7 = (f32[384,1536]{1,0:T(8,128)S(1)}, f32[384,1536]{1,0:T(8,128)}, u32[]{:S(2)}) copy-start(f32[384,1536]{1,0:T(8,128)} %get-tuple-element.31) | copy-start | bytes 7077892
  358.2 105.0 %reduce-scatter.5.cloned.1.call-start = ((), (), s32[]{:S(2)}) async-start(), calls=%async_computation.3 | async-start | bytes 5898240 | tf_op jit(solution)/shard_map/reduce_scatter | solution.py:242
  362.7 161.3 %all-reduce.8.cloned.1.call-start = ((), (), s32[]{:S(2)}) async-start(), calls=%async_computation.4 | async-start | bytes 2359296 | tf_op jit(solution)/shard_map/psum | solution.py:240
  376.9 86.2 %copy-start.21 = (f32[384]{0:T(512)S(1)}, f32[384]{0:T(512)}, u32[]{:S(2)}) copy-start(f32[384]{0:T(512)} %param.31) | copy-start | bytes 4612
  376.9 86.8 %copy-start.11 = (f32[54,96]{1,0:T(8,128)S(1)}, f32[54,96]{1,0:T(8,128)}, u32[]{:S(2)}) copy-start(f32[54,96]{1,0:T(8,128)} %param.24) | copy-start | bytes 62212
  376.9 86.8 %copy-start.12 = (f32[54,96]{1,0:T(8,128)S(1)}, f32[54,96]{1,0:T(8,128)}, u32[]{:S(2)}) copy-start(f32[54,96]{1,0:T(8,128)} %param.27) | copy-start | bytes 62212
  376.9 87.5 %copy-start.13 = (f32[54,96]{1,0:T(8,128)S(1)}, f32[54,96]{1,0:T(8,128)}, u32[]{:S(2)}) copy-start(f32[54,96]{1,0:T(8,128)} %param.30) | copy-start | bytes 62212
  382.0 142.0 %copy-start.4 = (f32[2,384,384]{2,1,0:T(8,128)S(1)}, f32[2,384,384]{2,1,0:T(8,128)}, u32[]{:S(2)}) copy-start(f32[2,384,384]{2,1,0:T(8,128)} %param.20) | copy-start | bytes 3538948
  407.6 120.7 %copy-start.14 = (f32[54,96]{1,0:T(8,128)}, f32[54,96]{1,0:T(8,128)S(1)}, u32[]{:S(2)}) copy-start(f32[54,96]{1,0:T(8,128)S(1)} %get-tuple-element.65) | copy-start | bytes 62212
  407.6 120.7 %copy-start.22 = (f32[384]{0:T(512)}, f32[384]{0:T(512)S(1)}, u32[]{:S(2)}) copy-start(f32[384]{0:T(512)S(1)} %get-tuple-element.66) | copy-start | bytes 4612
  408.2 120.0 %copy-start.16 = (f32[384]{0:T(512)}, f32[384]{0:T(512)S(1)}, u32[]{:S(2)}) copy-start(f32[384]{0:T(512)S(1)} %get-tuple-element.69) | copy-start | bytes 4612
  464.4 63.8 %copy-start.10 = (f32[54,96]{1,0:T(8,128)}, f32[54,96]{1,0:T(8,128)S(1)}, u32[]{:S(2)}) copy-start(f32[54,96]{1,0:T(8,128)S(1)} %get-tuple-element.68) | copy-start | bytes 62212
  465.0 63.2 %copy-start.8 = (f32[2,384,384]{2,1,0:T(8,128)S(1)}, f32[2,384,384]{2,1,0:T(8,128)}, u32[]{:S(2)}) copy-start(f32[2,384,384]{2,1,0:T(8,128)} %param.29) | copy-start | bytes 3538948
  (13 other events, 214.2 us)
Sparse Core Ops, SparseCore 0:
  14.6 54.9 all-gather.3
  358.3 18.9 reduce-scatter.6
  379.6 83.5 reduce-scatter.4
  466.2 57.7 all-reduce.7

commit v2 on v0

v2 whole, which is shorter than its diff:
```python
import functools

import jax
import jax.numpy as jnp
from jax import lax
from jax.experimental import pallas as pl
from jax.experimental.pallas import tpu as pltpu
from jax.sharding import PartitionSpec as P

C = 384
HID = 1536
KS = 7
R = KS // 2
STEP = 3
F32 = jnp.float32
BF = jnp.bfloat16


MESH = pl.DeviceIdType.MESH


def conv_group(xf, k_ref, cb_ref, z_ref):
    rows, cols = z_ref.shape[0], z_ref.shape[1]

    def step(t, _):
        hp = t // 3
        c = pl.ds(pl.multiple_of((t % 3) * 128, 128), 128)
        base = jnp.broadcast_to(cb_ref[0:1, c], (8, 128))
        acc = [[base] * cols for _ in range(2)]
        for ii in range(KS + 1):
            row = [xf[2 * hp + ii, w, :, c] for w in range(cols + KS - 1)]
            for r in range(2):
                i = ii - r
                if 0 <= i < KS:
                    for j in range(KS):
                        tap = k_ref[i * KS + j, :, c]
                        for w in range(cols):
                            acc[r][w] = acc[r][w] + row[w + j] * tap
        for r in range(2):
            for w in range(cols):
                z_ref[2 * hp + r, w, :, c] = acc[r][w]
        return 0

    lax.fori_loop(0, rows // 2 * 3, step, 0)


def conv_back_group(df, k_ref, xp, og, ig, gk, g):
    rows, cols = ig.shape[1], ig.shape[2]

    def step(t, _):
        h = t // 3
        c = pl.ds(pl.multiple_of((t % 3) * 128, 128), 128)
        x = [xp[g, h + R, w + R, :, c].astype(F32) for w in range(cols)]
        acc = [og[g, h, w, :, c].astype(F32) for w in range(cols)]
        for i in range(KS):
            row = [df[h + KS - 1 - i, w, :, c] for w in range(cols + KS - 1)]
            for j in range(KS):
                tap = k_ref[i * KS + j, :, c]
                part = None
                for w in range(cols):
                    d = row[w + KS - 1 - j]
                    acc[w] = acc[w] + d * tap
                    part = d * x[w] if part is None else part + d * x[w]
                gk[i * KS + j, :, c] = gk[i * KS + j, :, c] + part
        for w in range(cols):
            ig[g, h, w, :, c] = acc[w].astype(BF)
        return 0

    lax.fori_loop(0, rows * 3, step, 0)


def widen(src, g, dst):
    def step(t, _):
        for w in range(dst.shape[1]):
            dst[t, w] = src[g, t, w].astype(F32)
        return 0

    lax.fori_loop(0, dst.shape[0], step, 0)


def gelu_pair(v):
    t = 1.0 / (1.0 + (0.3275911 * 0.7071067811865476) * jnp.abs(v))
    e = jnp.exp(v * v * -0.5)
    tail = t * (0.127414796 + t * (-0.142248368 + t * (0.7107068705 + t * (-0.7265760135 + t * 0.5307027145)))) * e
    phi = jnp.where(v > 0, 1.0 - tail, tail)
    return v * phi, phi + v * e * 0.3989422804014327


def dg(a, b, ca, cb):
    return lax.dot_general(a, b, (((ca,), (cb,)), ((), ())), preferred_element_type=F32)


def mlp_group(z_ref, og, xp, gate_ref, wi, wo, bi_ref, ch_ref, out, dzp, gwi, gwo, gch, gbi, g):
    rows, cols = z_ref.shape[0], z_ref.shape[1]
    m = rows * cols * 8
    flat = lambda v: v.reshape(m, C)
    cube = lambda v: v.reshape(rows, cols, 8, C)
    gain, shift, bo, ls = (ch_ref[k : k + 1] for k in range(1, 5))
    z = flat(z_ref[...])
    zc = z - jnp.mean(z, axis=1, keepdims=True)
    inv = lax.rsqrt(jnp.mean(zc * zc, axis=1, keepdims=True) + 1e-6)
    xhat = zc * inv
    xn = (xhat * gain + shift).astype(BF)
    gate = gate_ref[g]
    gog = flat(og[g].astype(F32) * gate)
    db = (gog * ls).astype(BF)
    branch = jnp.zeros((m, C), F32)
    dxn = jnp.zeros((m, C), F32)
    for j in range(HID // HC):
        hs = slice(j * HC, (j + 1) * HC)
        pre = dg(xn, wi[:, hs], 1, 0) + bi_ref[0:1, hs]
        da = dg(db, wo[:, hs], 1, 0)
        act, slope = gelu_pair(pre)
        act = act.astype(BF)
        dpre = (da * slope).astype(BF)
        branch += dg(act, wo[:, hs], 1, 1)
        dxn += dg(dpre, wi[:, hs], 1, 1)
        gwo[:, hs] += dg(db, act, 0, 0)
        gwi[:, hs] += dg(xn, dpre, 0, 0)
        gbi[:, hs] += jnp.sum(dpre.astype(F32).reshape(m // 8, 8, HC), axis=0)
    branch += bo
    mid = (slice(R, R + rows), slice(R, R + cols))
    out[g] = (xp[(g, *mid)].astype(F32) + cube(ls * branch) * gate).astype(BF)
    q = dxn * gain
    m1 = jnp.mean(q, axis=1, keepdims=True)
    m2 = jnp.mean(q * xhat, axis=1, keepdims=True)
    dz = (inv * (q - m1 - xhat * m2)).astype(BF)
    dzp[(g, *mid)] = cube(dz)
    red = lambda v: jnp.sum(v.reshape(m // 8, 8, C), axis=0)
    gch[0] += red(dz.astype(F32))
    gch[1] += red(dxn * xhat)
    gch[2] += red(dxn)
    gch[3] += red(db.astype(F32))
    gch[4] += red(gog * branch)


HC = 512


def exchange(n_wa, rows, cols, pad, cs, cr, rs, rr):
    w = lax.axis_index("wa")
    a = lax.axis_index("ha")
    own = slice(R, R + rows)

    def to_left(g, src=None):
        src = pad.at[g, own, R : 2 * R] if src is None else src
        return pltpu.make_async_remote_copy(
            src, pad.at[g, own, R + cols :], cs.at[g, 0], cr.at[g, 0], device_id={"wa": w - 1}, device_id_type=MESH
        )

    def to_right(g, src=None):
        src = pad.at[g, own, cols : cols + R] if src is None else src
        return pltpu.make_async_remote_copy(
            src, pad.at[g, own, :R], cs.at[g, 1], cr.at[g, 1], device_id={"wa": w + 1}, device_id_type=MESH
        )

    def rows_to(g, up):
        src = pad.at[g, R : 2 * R] if up else pad.at[g, rows : rows + R]
        dst = pad.at[g, R + rows :] if up else pad.at[g, :R]
        return pltpu.make_async_remote_copy(
            src, dst, rs.at[g], rr.at[g], device_id={"ha": 1 - a}, device_id_type=MESH
        )

    def both(g, f0, f1):
        pl.when(a == 0)(lambda: f0(rows_to(g, False)))
        pl.when(a == 1)(lambda: f1(rows_to(g, True)))

    def start_cols(g, left=None, right=None):
        pl.when(w > 0)(lambda: to_left(g, left).start())
        pl.when(w < n_wa - 1)(lambda: to_right(g, right).start())

    def wait_cols(g):
        pl.when(w < n_wa - 1)(lambda: to_left(g).wait_recv())
        pl.when(w > 0)(lambda: to_right(g).wait_recv())

    def start_rows(g):
        both(g, lambda c: c.start(), lambda c: c.start())

    def wait_rows(g):
        rows_to(g, True).wait_recv()

    def drain(g):
        pl.when(w > 0)(lambda: to_left(g).wait_send())
        pl.when(w < n_wa - 1)(lambda: to_right(g).wait_send())
        rows_to(g, True).wait_send()

    def zero_edges(g):
        z = lambda h, v: jnp.zeros((h, v, 8, C), BF)
        pl.when(w == 0)(lambda: pad.__setitem__((g, own, slice(0, R)), z(rows, R)))
        pl.when(w == n_wa - 1)(lambda: pad.__setitem__((g, own, slice(R + cols, 2 * R + cols)), z(rows, R)))
        pl.when(a == 0)(lambda: pad.__setitem__((g, slice(0, R)), z(R, cols + 2 * R)))
        pl.when(a == 1)(lambda: pad.__setitem__((g, slice(R + rows, 2 * R + rows)), z(R, cols + 2 * R)))

    return start_cols, wait_cols, start_rows, wait_rows, drain, zero_edges


def main_kernel(
    n_wa, x_hbm, og_hbm, gate_ref, k_ref, ch_ref, bi_ref, wi, wo,
    out, ig, gwi, gwo, gch_out, gbi_out, gk_out,
    xp, dzp, og, xf, z, gch, gbi, gk,
    xcs, xcr, xrs, xrr, dcs, dcr, drs, drr, own_sem, og_sem,
):
    groups, rows, cols = x_hbm.shape[0], x_hbm.shape[1], x_hbm.shape[2]
    w = lax.axis_index("wa")
    a = lax.axis_index("ha")
    mid = (slice(R, R + rows), slice(R, R + cols))
    xh = exchange(n_wa, rows, cols, xp, xcs, xcr, xrs, xrr)
    dh = exchange(n_wa, rows, cols, dzp, dcs, dcr, drs, drr)
    own = lambda g: pltpu.make_async_copy(x_hbm.at[g], xp.at[(g, *mid)], own_sem.at[g])
    ogc = lambda g: pltpu.make_async_copy(og_hbm.at[g], og.at[g], og_sem.at[g])

    barrier = pltpu.get_barrier_semaphore()
    pl.when(w > 0)(lambda: pl.semaphore_signal(barrier, inc=1, device_id={"wa": w - 1}, device_id_type=MESH))
    pl.when(w < n_wa - 1)(lambda: pl.semaphore_signal(barrier, inc=1, device_id={"wa": w + 1}, device_id_type=MESH))
    pl.semaphore_signal(barrier, inc=1, device_id={"ha": 1 - a}, device_id_type=MESH)
    for g in range(groups):
        own(g).start()
        ogc(g).start()
    near = jnp.where(w > 0, 1, 0) + jnp.where(w < n_wa - 1, 1, 0) + 1
    pl.semaphore_wait(barrier, near)

    def loop(n, f):
        lax.fori_loop(0, n, lambda g, _: (f(g), 0)[1], 0)

    loop(groups, lambda g: xh[0](g, x_hbm.at[g, :, 0:R], x_hbm.at[g, :, cols - R : cols]))
    loop(groups, lambda g: (xh[5](g), dh[5](g)))
    gwi[...] = jnp.zeros_like(gwi)
    gwo[...] = jnp.zeros_like(gwo)
    gch[...] = jnp.zeros_like(gch)
    gbi[...] = jnp.zeros_like(gbi)
    gk[...] = jnp.zeros_like(gk)

    def ready(g):
        own(g).wait()
        xh[1](g)
        xh[2](g)

    ready(0)

    def forward(g):
        pl.when(g + 1 < groups)(lambda: ready(g + 1))
        xh[3](g)
        ogc(g).wait()
        widen(xp, g, xf)
        conv_group(xf, k_ref, ch_ref, z)
        mlp_group(z, og, xp, gate_ref, wi, wo, bi_ref, ch_ref, out, dzp, gwi, gwo, gch, gbi, g)
        dh[0](g)

    loop(groups, forward)

    def ready_back(g):
        dh[1](g)
        dh[2](g)

    ready_back(0)

    def backward(g):
        pl.when(g + 1 < groups)(lambda: ready_back(g + 1))
        dh[3](g)
        widen(dzp, g, xf)
        conv_back_group(xf, k_ref, xp, og, ig, gk, g)

    loop(groups, backward)
    gch_out[...] = jnp.sum(gch[...], axis=1)
    gbi_out[...] = jnp.sum(gbi[...], axis=0, keepdims=True)
    gk_out[...] = jnp.sum(gk[...], axis=1)
    loop(groups, lambda g: (xh[4](g), dh[4](g)))


def run_main(n_wa, x, og, gate, taps, ch, bi, wi, wo):
    groups, rows, cols = x.shape[:3]
    hbm = pl.BlockSpec(memory_space=pl.ANY)
    vm = pl.BlockSpec(memory_space=pltpu.VMEM)
    big = (groups, rows + 2 * R, cols + 2 * R, 8, C)
    dma = pltpu.SemaphoreType.DMA
    S = jax.ShapeDtypeStruct
    return pl.pallas_call(
        functools.partial(main_kernel, n_wa),
        out_shape=(S(x.shape, BF), S(x.shape, BF), S((C, HID), F32), S((C, HID), F32), S((8, C), F32), S((1, HID), F32), S((49, C), F32)),
        in_specs=[hbm, hbm] + [vm] * 6,
        out_specs=(vm,) * 7,
        scratch_shapes=[
            pltpu.VMEM(big, BF), pltpu.VMEM(big, BF), pltpu.VMEM(x.shape, BF),
            pltpu.VMEM(big[1:], F32), pltpu.VMEM((rows, cols, 8, C), F32),
            pltpu.VMEM((8, 8, C), F32), pltpu.VMEM((8, HID), F32), pltpu.VMEM((49, 8, C), F32),
            dma((groups, 2)), dma((groups, 2)), dma((groups,)), dma((groups,)),
            dma((groups, 2)), dma((groups, 2)), dma((groups,)), dma((groups,)),
            dma((groups,)), dma((groups,)),
        ],
        compiler_params=pltpu.CompilerParams(collective_id=0, has_side_effects=True, vmem_limit_bytes=67043328),
        name="main",
    )(x, og, gate, taps, ch, bi, wi, wo)


def adam_step(master, grad, moment, second, average, rate):
    moment_new = 0.5 * moment + 0.5 * grad
    second_new = 0.5 * second + 0.5 * grad * grad
    correct = 1.0 - 0.5**STEP
    master_new = master - rate * (
        moment_new / correct / (jnp.sqrt(second_new / correct) + 1e-08) + 0.05 * master
    )
    average_new = 0.9 * average + 0.1 * master_new
    return (master_new, moment_new, second_new, average_new)


def local(
    images,
    out_grad,
    keep_mask,
    img_counts,
    mats_master,
    chan_master,
    bias_master,
    mats_moment,
    chan_moment,
    bias_moment,
    mats_second,
    chan_second,
    bias_second,
    mats_average,
    chan_average,
    bias_average,
):
    n_img, rows, cols = images.shape[0], images.shape[1], images.shape[2]
    groups = -(-n_img // 8)
    slots = groups * 8
    mats_all, chan_all, bias_all = (
        lax.all_gather(mats_master.astype(BF), "ba", axis=2, tiled=True),
        lax.all_gather(chan_master.astype(BF), "ba", axis=1, tiled=True),
        lax.all_gather(bias_master.astype(BF), "ba", axis=0, tiled=True),
    )
    chan_vals = chan_all.astype(F32)
    taps, rest = chan_vals[:49], jnp.pad(chan_vals[49:], ((0, 3), (0, 0)))
    fill = jnp.arange(n_img, dtype=jnp.int32) < img_counts[0]
    gate = jnp.pad(jnp.where(fill, keep_mask, 0).astype(F32), (0, slots - n_img))
    gate = jnp.broadcast_to(gate.reshape(groups, 8, 1), (groups, 8, C))

    def grouped(v):
        v = jnp.pad(v.transpose(1, 2, 0, 3), ((0, 0), (0, 0), (0, slots - n_img), (0, 0)))
        return v.reshape(rows, cols, groups, 8, C).transpose(2, 0, 1, 3, 4)

    out, ig, grad_win, grad_wout, gch, gbi, grad_taps = run_main(
        lax.axis_size("wa"), grouped(images), grouped(out_grad), gate, taps[:, None],
        rest, bias_all.astype(F32)[None], mats_all[0], mats_all[1],
    )
    back = lambda v: v.transpose(1, 2, 0, 3, 4).reshape(rows, cols, slots, C)[:, :, :n_img].transpose(2, 0, 1, 3)
    outputs, input_grad = back(out), back(ig)
    mats_local = jnp.stack([grad_win, grad_wout], axis=0)
    chan_local = jnp.concatenate([grad_taps, gch[:5]], axis=0)
    grad_hbias = gbi[0]
    whole = lax.psum((mats_local, chan_local, grad_hbias), ("ha", "wa"))
    mats_grad, chan_grad, bias_grad = (
        lax.psum_scatter(whole[0], "ba", scatter_dimension=2, tiled=True),
        lax.psum_scatter(whole[1], "ba", scatter_dimension=1, tiled=True),
        lax.psum_scatter(whole[2], "ba", scatter_dimension=0, tiled=True),
    )
    mats_new, mats_moment_new, mats_second_new, mats_average_new = adam_step(
        mats_master, mats_grad, mats_moment, mats_second, mats_average, 0.03
    )
    chan_new, chan_moment_new, chan_second_new, chan_average_new = adam_step(
        chan_master, chan_grad, chan_moment, chan_second, chan_average, 0.3
    )
    bias_new, bias_moment_new, bias_second_new, bias_average_new = adam_step(
        bias_master, bias_grad, bias_moment, bias_second, bias_average, 0.3
    )
    return (
        outputs,
        input_grad,
        mats_grad,
        chan_grad,
        bias_grad,
        mats_new,
        chan_new,
        bias_new,
        mats_moment_new,
        chan_moment_new,
        bias_moment_new,
        mats_second_new,
        chan_second_new,
        bias_second_new,
        mats_average_new,
        chan_average_new,
        bias_average_new,
        mats_new.astype(jnp.bfloat16),
        chan_new.astype(jnp.bfloat16),
        bias_new.astype(jnp.bfloat16),
    )


def solution(mesh):
    return jax.shard_map(
        local,
        mesh=mesh,
        in_specs=(
            P("ba", "ha", "wa", None),
            P("ba", "ha", "wa", None),
            P("ba"),
            P("ba"),
            P(None, None, "ba"),
            P(None, "ba"),
            P("ba"),
            P(None, None, "ba"),
            P(None, "ba"),
            P("ba"),
            P(None, None, "ba"),
            P(None, "ba"),
            P("ba"),
            P(None, None, "ba"),
            P(None, "ba"),
            P("ba"),
        ),
        out_specs=(
            P("ba", "ha", "wa", None),
            P("ba", "ha", "wa", None),
            P(None, None, "ba"),
            P(None, "ba"),
            P("ba"),
            P(None, None, "ba"),
            P(None, "ba"),
            P("ba"),
            P(None, None, "ba"),
            P(None, "ba"),
            P("ba"),
            P(None, None, "ba"),
            P(None, "ba"),
            P("ba"),
            P(None, None, "ba"),
            P(None, "ba"),
            P("ba"),
            P(None, None, "ba"),
            P(None, "ba"),
            P("ba"),
        ),
        check_vma=False,
    )
```

time: 590 us -> 396 us (0.67)
  other arithmetic: 189 us -> 18.8 us
  Pallas kernels: 0 us -> 143 us
  matrix products: 108 us -> 0 us
  waiting for transfers between devices: 66.2 us -> 129 us
  blocking collectives: 129 us -> 67.6 us
  local copies, waits for them, and re-layouts: 54.4 us -> 21.4 us
  starting transfers between devices: 22.3 us -> 0.16 us
    pallas_call x0 -> x1, Pallas kernels: none -> 143 us  [run_main(): pl.pallas_call(functools.partial(main_kernel, n_wa), out_shape=(S(x.shape...]
    reduce_sum x9 -> x0, other arithmetic: 113 us -> none  [the longest x1 59.9 us: local(): center = conv - jnp.mean(conv, axis=-1, keepdims=True)]
    dot_general x6 -> x0, matrix products: 108 us -> none  [the longest x1 46 us: local(): jnp.dot(flat_in, w_in, preferred_element_type=jnp.float32) + hid_bias]
    psum x1, blocking collectives: 89.7 us -> 30.2 us  [local(): whole = lax.psum((mats_local, chan_local, grad_hbias), ('ha', 'wa'))]
    ppermute x8 -> x0, waiting for transfers between devices: 57.3 us -> none  [the longest x4 45.6 us: with_halo(): lax.ppermute(head, axis, [((i + 1) % count, i) for i in range(ends)])]
    reduce_scatter x1, waiting for transfers between devices: 0.02 us -> 52.8 us  [local(): lax.psum_scatter(whole[0], 'ba', scatter_dimension=2, tiled=True)]
    convert_element_type x6 -> x3, other arithmetic: 51.9 us -> 2.31 us  [the longest x1 2.3 us: local(): mats_master.astype(BF)]
    psum x1, waiting for transfers between devices: 8.79 us -> 56.1 us  [local(): whole = lax.psum((mats_local, chan_local, grad_hbias), ('ha', 'wa'))]
  transfers between devices with their start and end apart: 12 -> 4, of which waited for: 6 -> 4; matrix products, arithmetic and copies ran while one was open for 24% -> 6% of each run, Pallas kernels for 0% -> 0%
where the time goes in v2:
time: 396 us; the launch traced here: 395 us
  Pallas kernels  143 us (36%)
  waiting for transfers between devices  129 us (33%)
  blocking collectives  67.6 us (17%)
  local copies, waits for them, and re-layouts  21.4 us (5%)
  other arithmetic  18.8 us (5%)
  between operations  15.3 us (4%)
    pallas_call x1, Pallas kernels, run_main(): pl.pallas_call(functools.partial(main_kernel, n_wa), out_shape=(S(x.shape...  143 us
    psum x1, waiting for transfers between devices, local(): whole = lax.psum((mats_local, chan_local, grad_hbias), ('ha', 'wa'))  56.1 us
    reduce_scatter x1, waiting for transfers between devices, local(): lax.psum_scatter(whole[0], 'ba', scatter_dimension=2, tiled=True)  52.8 us
    psum x1, blocking collectives, local(): whole = lax.psum((mats_local, chan_local, grad_hbias), ('ha', 'wa'))  30.2 us
    all_gather x1, waiting for transfers between devices, local(): lax.all_gather(mats_master.astype(BF), 'ba', axis=2, tiled=True)  18.6 us
    all_gather x1, blocking collectives, local(): lax.all_gather(chan_master.astype(BF), 'ba', axis=1, tiled=True)  14.9 us
    all_gather x1, blocking collectives, local(): lax.all_gather(bias_master.astype(BF), 'ba', axis=0, tiled=True)  12.6 us
    unnamed x1, blocking collectives  9.89 us
  transfers between devices with their start and end apart: 4, of which 4 were waited for; matrix products, arithmetic and copies ran while one was open for 6% of the time, Pallas kernels for 0%

profile of v2, /device:TPU:0, one launch (start us, length us, event | category | flops | bytes accessed | tf_op | source)
XLA Modules:
  0.0 394.9 jit_solution(4889680307374561086)
XLA Ops:
  7.3 2.3 convert_element_type.36
  9.7 14.9 %all-gather = bf16[4,96,54]{1,2,0:T(8,128)(2,1)S(1)} all-gather(bf16[1,96,54]{1,2,0:T(8,128)(2,1)S(1)} %convert_bitcast_fusion), channel_id=1, replica_groups=mesh['ha'=2,'wa'=4,'ba'=4] {'ba'}, dimensions={0}, use_global_device_ids=true | all-gather | bytes 51840 | tf_op jit(solution)/shard_map/all_gather | solution.py:329
  26.8 12.6 %all-gather.1 = bf16[4,1,384]{2,1,0:T(2,128)(2,1)S(1)} all-gather(bf16[1,1,384]{2,1,0:T(2,128)(2,1)S(1)} %reshape.61), channel_id=1, replica_groups=mesh['ha'=2,'wa'=4,'ba'=4] {'ba'}, dimensions={0}, use_global_device_ids=true | all-gather | bytes 3840 | tf_op jit(solution)/shard_map/all_gather | solution.py:330
  40.0 4.8 %copy_bitcast_fusion.2 = (bf16[6,12,6,8,384]{4,3,2,1,0:T(8,128)(2,1)}, bf16[6,12,6,8,384]{4,3,2,1,0:T(8,128)(2,1)}) fusion(bf16[12,6,42,384]{3,2,1,0:T(8,128)(2,1)S(1)} %bitcast.49, bf16[12,6,42,384]{3,2,1,0:T(8,128)(2,1)} %bitcast.50), kind=kLoop, calls=%fused_computation.5 | loop fusion | bytes 9953280 | tf_op jit(solution)/shard_map/transpose | solution.py:340
  44.8 18.6 %all-gather.4.cloned.1.call-done = bf16[2,384,1536]{2,1,0:T(8,128)(2,1)} async-done(((bf16[2,384,384]{2,1,0:T(8,128)(2,1)}), bf16[2,384,1536]{2,1,0:T(8,128)(2,1)}) %all-gather.4.cloned.1.call-update) | async-done | bytes 2359312 | tf_op jit(solution)/shard_map/all_gather | solution.py:328
  63.3 3.2 slice_bitcast_fusion.2
  67.2 142.6 %main.1 = (bf16[6,12,6,8,384]{4,3,2,1,0:T(8,128)(2,1)}, bf16[6,12,6,8,384]{4,3,2,1,0:T(8,128)(2,1)}, f32[384,1536]{1,0:T(8,128)}, f32[384,1536]{1,0:T(8,128)}, f...) custom-call(bf16[6,12,6,8,384]{4,3,2,1,0:T(8,128)(2,1)} %get-tuple-element.51.x_hbm, ...), custom_call_target="tpu_custom_call" | custom-call | tf_op jit(solution)/shard_map/main/pallas_call | solution.py:277
  211.6 4.8 %pad_maximum_fusion = f32[2,384,1536]{2,1,0:T(8,128)} fusion(f32[1,384,1536]{2,1,0:T(8,128)} %bitcast.52, f32[1,384,1536]{2,1,0:T(8,128)} %bitcast.51), kind=kLoop, calls=%fused_computation | loop fusion | flops 1179648 | bytes 9437184 | tf_op jit(solution)/shard_map/stack | solution.py:348
  218.4 9.9 %all-reduce.4 = f32[1536]{0:T(1024)S(1)} all-reduce(f32[1536]{0:T(1024)S(1)} %reduce), channel_id=4, replica_groups=mesh['ha'=2,'wa'=4,'ba'=4] {'ba'}, use_global_device_ids=true, to_apply=%region_5.6.clone | all-reduce | flops 1536 | bytes 12288
  228.6 1.8 slice_bitcast_fusion
  230.4 0.9 copy-done.3
  231.7 1.8 slice_bitcast_fusion.1
  233.5 1.4 reduce-scatter.7.cloned.1.call-done
  234.9 1.5 copy.51
  236.4 30.2 %all-reduce.5 = (f32[54,96]{1,0:T(8,128)}, f32[384]{0:T(512)}) all-reduce(f32[54,96]{1,0:T(8,128)} %copy.51, f32[384]{0:T(512)S(1)} %dynamic-slice.1), channel_id=1, replica_groups=mesh['ha'=2,'wa'=4,'ba'=4] {'ha','wa'}, use_global_device_ids=true, to_apply=%region_2.3 | all-reduce | flops 5568 | bytes 44544 | tf_op jit(solution)/shard_map/psum | solution.py:351
  266.6 1.3 fusion.4
  267.9 52.8 %reduce-scatter.5.cloned.1.call-done = f32[2,384,384]{2,1,0:T(8,128)} async-done(((f32[2,384,1536]{2,1,0:T(8,128)}), f32[2,384,384]{2,1,0:T(8,128)}) %reduce-scatter.5.cloned.1.call-update) | async-done | bytes 1179664 | tf_op jit(solution)/shard_map/reduce_scatter | solution.py:353
  320.8 1.3 multiply_add_fusion.5
  322.0 1.4 fusion.6
  324.1 1.4 multiply_add_fusion.3
  325.4 56.1 %all-reduce.8.cloned.1.call-done = f32[2,384,384]{2,1,0:T(8,128)} async-done(((f32[2,384,384]{2,1,0:T(8,128)}), f32[2,384,384]{2,1,0:T(8,128)}) %all-reduce.8.cloned.1.call-update) | async-done | bytes 1179664 | tf_op jit(solution)/shard_map/psum | solution.py:351
  381.6 3.6 fusion.8
  385.2 1.2 multiply_add_fusion.1
  387.3 1.0 copy.58
  (66 shorter events, 8.2 us)
Async XLA Ops:
  7.2 2.5 copy-start.9
  7.2 19.5 %copy-start.17 = (s32[42]{0:T(128)S(1)}, s32[42]{0:T(128)}, u32[]{:S(2)}) copy-start(s32[42]{0:T(128)} %param.18) | copy-start | bytes 508
  7.2 19.6 %copy-start.12 = (f32[384]{0:T(512)S(1)}, f32[384]{0:T(512)}, u32[]{:S(2)}) copy-start(f32[384]{0:T(512)} %param.22) | copy-start | bytes 4612
  7.2 56.1 %all-gather.4.cloned.1.call-start = ((), (), s32[]{:S(2)}) async-start(), calls=%async_computation.2 | async-start | bytes 2949120 | tf_op jit(solution)/shard_map/all_gather | solution.py:328
  7.3 32.7 %copy-start.5 = (bf16[42,12,6,384]{3,0,2,1:T(8,128)(2,1)S(1)}, bf16[42,12,6,384]{3,0,2,1:T(8,128)(2,1)}, u32[]{:S(2)}) copy-start(bf16[42,12,6,384]{3,0,2,1:T(8,128)(2,1)} %param.16) | copy-start | bytes 6967300
  9.6 225.3 %reduce-scatter.7.cloned.1.call-start = ((), (), s32[]{:S(2)}) async-start(), calls=%async_computation.5 | async-start | bytes 245760
  211.6 109.2 %reduce-scatter.5.cloned.1.call-start = ((), (), s32[]{:S(2)}) async-start(), calls=%async_computation.3 | async-start | bytes 5898240 | tf_op jit(solution)/shard_map/reduce_scatter | solution.py:353
  216.5 0.7 copy-start.18
  216.5 1.9 copy-start.14
  216.5 11.9 %copy-start.4 = (bf16[6,12,6,8,384]{4,3,2,1,0:T(8,128)(2,1)S(1)}, bf16[6,12,6,8,384]{4,3,2,1,0:T(8,128)(2,1)}, u32[]{:S(2)}) copy-start(bf16[6,12,6,8,384]{4,3,2,1,0:T(8,128)(2,1)} %get-tuple-element.28) | copy-start | bytes 7962628
  216.5 165.1 %all-reduce.8.cloned.1.call-start = ((), (), s32[]{:S(2)}) async-start(), calls=%async_computation.4 | async-start | bytes 2359296 | tf_op jit(solution)/shard_map/psum | solution.py:351
  228.6 2.7 copy-start.3
  231.6 35.0 %copy-start.13 = (f32[384]{0:T(512)S(1)}, f32[384]{0:T(512)}, u32[]{:S(2)}) copy-start(f32[384]{0:T(512)} %param.22) | copy-start | bytes 4612
  231.6 35.0 %copy-start.15 = (f32[384]{0:T(512)S(1)}, f32[384]{0:T(512)}, u32[]{:S(2)}) copy-start(f32[384]{0:T(512)} %param.25) | copy-start | bytes 4612
  231.7 35.0 %copy-start.16 = (f32[384]{0:T(512)S(1)}, f32[384]{0:T(512)}, u32[]{:S(2)}) copy-start(f32[384]{0:T(512)} %param.28) | copy-start | bytes 4612
  231.7 149.9 %copy-start.6 = (f32[2,384,384]{2,1,0:T(8,128)S(1)}, f32[2,384,384]{2,1,0:T(8,128)}, u32[]{:S(2)}) copy-start(f32[2,384,384]{2,1,0:T(8,128)} %param.23) | copy-start | bytes 3538948
  231.7 149.9 %copy-start.7 = (f32[2,384,384]{2,1,0:T(8,128)S(1)}, f32[2,384,384]{2,1,0:T(8,128)}, u32[]{:S(2)}) copy-start(f32[2,384,384]{2,1,0:T(8,128)} %param.26) | copy-start | bytes 3538948
  233.5 148.1 %copy-start.1 = (f32[2,384,384]{2,1,0:T(8,128)S(1)}, f32[2,384,384]{2,1,0:T(8,128)}, u32[]{:S(2)}) copy-start(f32[2,384,384]{2,1,0:T(8,128)} %param.20) | copy-start | bytes 3538948
  267.9 117.3 %copy-start.11 = (f32[384]{0:T(512)}, f32[384]{0:T(512)S(1)}, u32[]{:S(2)}) copy-start(f32[384]{0:T(512)S(1)} %get-tuple-element.59) | copy-start | bytes 4612
  323.5 0.6 copy-start.10
  381.6 3.6 copy-start.8
  385.2 1.4 copy-start
  385.2 2.1 copy-start.2
Sparse Core Ops, SparseCore 0:
  10.2 53.0 all-gather.3
  211.7 23.1 reduce-scatter.6
  237.2 83.5 reduce-scatter.4
  323.8 57.7 all-reduce.7

commit v3 on v2

--- a/solution.py
+++ b/solution.py
@@ -19,13 +19,13 @@
 MESH = pl.DeviceIdType.MESH
 
 
-def conv_group(xf, k_ref, cb_ref, z_ref):
+def conv_group(xf, ch, z_ref):
     rows, cols = z_ref.shape[0], z_ref.shape[1]
 
     def step(t, _):
         hp = t // 3
         c = pl.ds(pl.multiple_of((t % 3) * 128, 128), 128)
-        base = jnp.broadcast_to(cb_ref[0:1, c], (8, 128))
+        base = jnp.broadcast_to(ch[49:50, c], (8, 128))
         acc = [[base] * cols for _ in range(2)]
         for ii in range(KS + 1):
             row = [xf[2 * hp + ii, w, :, c] for w in range(cols + KS - 1)]
@@ -33,7 +33,7 @@
                 i = ii - r
                 if 0 <= i < KS:
                     for j in range(KS):
-                        tap = k_ref[i * KS + j, :, c]
+                        tap = ch[i * KS + j : i * KS + j + 1, c]
                         for w in range(cols):
                             acc[r][w] = acc[r][w] + row[w + j] * tap
         for r in range(2):
@@ -44,18 +44,18 @@
     lax.fori_loop(0, rows // 2 * 3, step, 0)
 
 
-def conv_back_group(df, k_ref, xp, og, ig, gk, g):
+def conv_back_group(df, ch, xp, og, ig, gk, g, first, count):
     rows, cols = ig.shape[1], ig.shape[2]
 
     def step(t, _):
-        h = t // 3
+        h = first + t // 3
         c = pl.ds(pl.multiple_of((t % 3) * 128, 128), 128)
         x = [xp[g, h + R, w + R, :, c].astype(F32) for w in range(cols)]
         acc = [og[g, h, w, :, c].astype(F32) for w in range(cols)]
         for i in range(KS):
             row = [df[h + KS - 1 - i, w, :, c] for w in range(cols + KS - 1)]
             for j in range(KS):
-                tap = k_ref[i * KS + j, :, c]
+                tap = ch[i * KS + j : i * KS + j + 1, c]
                 part = None
                 for w in range(cols):
                     d = row[w + KS - 1 - j]
@@ -66,7 +66,7 @@
             ig[g, h, w, :, c] = acc[w].astype(BF)
         return 0
 
-    lax.fori_loop(0, rows * 3, step, 0)
+    lax.fori_loop(0, count * 3, step, 0)
 
 
 def widen(src, g, dst):
@@ -90,12 +90,12 @@
     return lax.dot_general(a, b, (((ca,), (cb,)), ((), ())), preferred_element_type=F32)
 
 
-def mlp_group(z_ref, og, xp, gate_ref, wi, wo, bi_ref, ch_ref, out, dzp, gwi, gwo, gch, gbi, g):
+def mlp_group(z_ref, og, xp, gate_ref, w_all, bi_ref, ch_ref, out, dzp, gw, gch, gbi, g):
     rows, cols = z_ref.shape[0], z_ref.shape[1]
     m = rows * cols * 8
     flat = lambda v: v.reshape(m, C)
     cube = lambda v: v.reshape(rows, cols, 8, C)
-    gain, shift, bo, ls = (ch_ref[k : k + 1] for k in range(1, 5))
+    gain, shift, bo, ls = (ch_ref[k : k + 1] for k in range(50, 54))
     z = flat(z_ref[...])
     zc = z - jnp.mean(z, axis=1, keepdims=True)
     inv = lax.rsqrt(jnp.mean(zc * zc, axis=1, keepdims=True) + 1e-6)
@@ -108,15 +108,15 @@
     dxn = jnp.zeros((m, C), F32)
     for j in range(HID // HC):
         hs = slice(j * HC, (j + 1) * HC)
-        pre = dg(xn, wi[:, hs], 1, 0) + bi_ref[0:1, hs]
-        da = dg(db, wo[:, hs], 1, 0)
+        pre = dg(xn, w_all[0, :, hs], 1, 0) + bi_ref[0:1, hs]
+        da = dg(db, w_all[1, :, hs], 1, 0)
         act, slope = gelu_pair(pre)
         act = act.astype(BF)
         dpre = (da * slope).astype(BF)
-        branch += dg(act, wo[:, hs], 1, 1)
-        dxn += dg(dpre, wi[:, hs], 1, 1)
-        gwo[:, hs] += dg(db, act, 0, 0)
-        gwi[:, hs] += dg(xn, dpre, 0, 0)
+        branch += dg(act, w_all[1, :, hs], 1, 1)
+        dxn += dg(dpre, w_all[0, :, hs], 1, 1)
+        gw[1, :, hs] += dg(db, act, 0, 0)
+        gw[0, :, hs] += dg(xn, dpre, 0, 0)
         gbi[:, hs] += jnp.sum(dpre.astype(F32).reshape(m // 8, 8, HC), axis=0)
     branch += bo
     mid = (slice(R, R + rows), slice(R, R + cols))
@@ -194,102 +194,369 @@
     return start_cols, wait_cols, start_rows, wait_rows, drain, zero_edges
 
 
-def main_kernel(
-    n_wa, x_hbm, og_hbm, gate_ref, k_ref, ch_ref, bi_ref, wi, wo,
-    out, ig, gwi, gwo, gch_out, gbi_out, gk_out,
-    xp, dzp, og, xf, z, gch, gbi, gk,
-    xcs, xcr, xrs, xrr, dcs, dcr, drs, drr, own_sem, og_sem,
-):
+def place(b, shape, axis):
+    whole = lax.broadcasted_iota(jnp.int32, shape, axis)
+    part = lax.broadcasted_iota(jnp.int32, shape, 1 - axis)
+    return jnp.where((whole == part + b * 96) & (part < 96), 1.0, 0.0).astype(BF)
+
+
+def remote(src, dst, send, recv, **where):
+    return pltpu.make_async_remote_copy(src, dst, send, recv, device_id=where, device_id_type=MESH)
+
+
+def main_kernel(n_wa, n_ba, *refs):
+    inside = n_ba == 4
+    it = iter(refs)
+    take = lambda n: [next(it) for _ in range(n)]
+    x_hbm, og_hbm, gate_ref = take(3)
+    if inside:
+        mats_hbm, small_hbm = take(2)
+    else:
+        w_all, ch, bi = take(3)
+    out, ig = take(2)
+    if inside:
+        gf, gsmall = take(2)
+    else:
+        gw, gch_out, gbi_out, gk_out = take(4)
+    xp, dzp, og, xf, z, gch, gbi, gk = take(8)
+    xcs, xcr, xrs, xrr, dcs, dcr, drs, drr, own_sem, og_sem = take(10)
+    if inside:
+        w_all, ch, bi, gw, s_all = take(5)
+        s_send, s_recv, w_own, w_up, w_dn, w_recv, w_cs, w_cr = take(8)
+        sb, rb, ub, db, ui, di, fin, pb, pi = take(9)
+        r_cs, r_cr, u_s, u_r, d_s, d_r, p_s, p_r, q_s, q_r, f_s, f_r = take(12)
+        gs, gs_in, gp, gz, gz_out = take(5)
+        t_s, t_r, tp_s, tp_r, tz_s, tz_r = take(6)
+
     groups, rows, cols = x_hbm.shape[0], x_hbm.shape[1], x_hbm.shape[2]
     w = lax.axis_index("wa")
     a = lax.axis_index("ha")
+    me = lax.axis_index("ba")
     mid = (slice(R, R + rows), slice(R, R + cols))
     xh = exchange(n_wa, rows, cols, xp, xcs, xcr, xrs, xrr)
     dh = exchange(n_wa, rows, cols, dzp, dcs, dcr, drs, drr)
     own = lambda g: pltpu.make_async_copy(x_hbm.at[g], xp.at[(g, *mid)], own_sem.at[g])
     ogc = lambda g: pltpu.make_async_copy(og_hbm.at[g], og.at[g], og_sem.at[g])
 
+    def loop(n, f):
+        lax.fori_loop(0, n, lambda g, _: (f(g), 0)[1], 0)
+
+    def when(cond, f):
+        pl.when(cond)(f)
+
     barrier = pltpu.get_barrier_semaphore()
-    pl.when(w > 0)(lambda: pl.semaphore_signal(barrier, inc=1, device_id={"wa": w - 1}, device_id_type=MESH))
-    pl.when(w < n_wa - 1)(lambda: pl.semaphore_signal(barrier, inc=1, device_id={"wa": w + 1}, device_id_type=MESH))
-    pl.semaphore_signal(barrier, inc=1, device_id={"ha": 1 - a}, device_id_type=MESH)
+    greet = lambda **d: pl.semaphore_signal(barrier, inc=1, device_id=d, device_id_type=MESH)
     for g in range(groups):
         own(g).start()
         ogc(g).start()
-    near = jnp.where(w > 0, 1, 0) + jnp.where(w < n_wa - 1, 1, 0) + 1
-    pl.semaphore_wait(barrier, near)
-
-    def loop(n, f):
-        lax.fori_loop(0, n, lambda g, _: (f(g), 0)[1], 0)
-
-    loop(groups, lambda g: xh[0](g, x_hbm.at[g, :, 0:R], x_hbm.at[g, :, cols - R : cols]))
+    greet(ha=1 - a)
+    if inside:
+        for d in range(1, n_wa):
+            greet(wa=lax.rem(w + d, n_wa))
+        for d in range(1, n_ba):
+            greet(ba=lax.rem(me + d, n_ba))
+        pl.semaphore_wait(barrier, n_wa + n_ba - 1)
+    else:
+        when(w > 0, lambda: greet(wa=w - 1))
+        when(w < n_wa - 1, lambda: greet(wa=w + 1))
+        pl.semaphore_wait(barrier, jnp.where(w > 0, 1, 0) + jnp.where(w < n_wa - 1, 1, 0) + 1)
+
+    xh[0](0, x_hbm.at[0, :, 0:R], x_hbm.at[0, :, cols - R : cols])
+    if inside:
+        lanes = lambda s: pl.ds(pl.multiple_of(s * C, C), C)
+        shard = lambda h, s: w_all.at[h, :, lanes(s)]
+        small_to = lambda d: remote(
+            small_hbm, s_all.at[me], s_send.at[d - 1], s_recv.at[me], ba=lax.rem(me + d, n_ba)
+        )
+        small_from = lambda s: remote(small_hbm, s_all.at[s], s_send.at[0], s_recv.at[s], ba=me)
+        w_mine = lambda h: pltpu.make_async_copy(mats_hbm.at[h], shard(h, me), w_own.at[h])
+        s_mine = pltpu.make_async_copy(small_hbm, s_all.at[me], w_own.at[2])
+        w_up_to = lambda s, src: remote(src, shard(a, s), w_up.at[s], w_recv.at[s], ba=me + 1)
+        w_dn_to = lambda s, src: remote(src, shard(a, s), w_dn.at[s], w_recv.at[s], ba=me - 1)
+        w_core = lambda s: remote(shard(a, s), shard(a, s), w_cs.at[s], w_cr.at[s], ha=1 - a)
+        for d in range(1, n_ba):
+            small_to(d).start()
+        when(me < n_ba - 1, lambda: w_up_to(me, mats_hbm.at[a]).start())
+        when(me > 0, lambda: w_dn_to(me, mats_hbm.at[a]).start())
+        s_mine.start()
+        w_mine(0).start()
+        w_mine(1).start()
+
+        def hop(d):
+            def low():
+                w_up_to(me - d, shard(a, me - d)).wait_recv()
+                when(me < n_ba - 1, lambda: w_up_to(me - d, shard(a, me - d)).start())
+                w_core(me - d).start()
+
+            def high():
+                w_dn_to(me + d, shard(a, me + d)).wait_recv()
+                when(me > 0, lambda: w_dn_to(me + d, shard(a, me + d)).start())
+                w_core(me + d).start()
+
+            when(me >= d, low)
+            when(me + d < n_ba, high)
+
+    loop(groups - 1, lambda g: xh[0](g + 1, x_hbm.at[g + 1, :, 0:R], x_hbm.at[g + 1, :, cols - R : cols]))
     loop(groups, lambda g: (xh[5](g), dh[5](g)))
-    gwi[...] = jnp.zeros_like(gwi)
-    gwo[...] = jnp.zeros_like(gwo)
+    gw[...] = jnp.zeros_like(gw)
     gch[...] = jnp.zeros_like(gch)
     gbi[...] = jnp.zeros_like(gbi)
     gk[...] = jnp.zeros_like(gk)
+    if inside:
+        s_mine.wait()
+        for d in range(1, n_ba):
+            small_from(lax.rem(me + d, n_ba)).wait_recv()
+        ch[...] = sum(dg(s_all[b], place(b, (128, C), 1), 1, 0) for b in range(n_ba))
+        for b in range(n_ba):
+            part = s_all[b, 56:64].astype(F32)
+            for k in range(3):
+                bi[0:1, b * C + k * 128 : b * C + (k + 1) * 128] = part[k : k + 1]
 
     def ready(g):
         own(g).wait()
         xh[1](g)
         xh[2](g)
 
+    def conv(g):
+        when(g + 1 < groups, lambda: ready(g + 1))
+        xh[3](g)
+        widen(xp, g, xf)
+        conv_group(xf, ch, z.at[g % 2])
+
     ready(0)
+    if inside:
+        hop(1)
+    conv(0)
+    if inside:
+        hop(2)
+    conv(1)
+    if inside:
+        hop(3)
+        w_mine(0).wait()
+        w_mine(1).wait()
+        for d in range(1, n_ba):
+            w_core(lax.rem(me + d, n_ba)).wait_recv()
 
     def forward(g):
-        pl.when(g + 1 < groups)(lambda: ready(g + 1))
-        xh[3](g)
         ogc(g).wait()
-        widen(xp, g, xf)
-        conv_group(xf, k_ref, ch_ref, z)
-        mlp_group(z, og, xp, gate_ref, wi, wo, bi_ref, ch_ref, out, dzp, gwi, gwo, gch, gbi, g)
+        mlp_group(z.at[g % 2], og, xp, gate_ref, w_all, bi, ch, out, dzp, gw, gch, gbi, g)
         dh[0](g)
+        when(g + 2 < groups, lambda: conv(g + 2))
 
     loop(groups, forward)
+
+    actions = []
+    if inside:
+        part = lambda s: slice(s * C, (s + 1) * C)
+        to_core = lambda s: remote(sb.at[s], rb.at[s], r_cs.at[s], r_cr.at[s], ha=1 - a)
+        up = lambda s: remote(ub.at[s], ui.at[s], u_s.at[s], u_r.at[s], ba=me + 1)
+        down = lambda s: remote(db.at[s], di.at[s], d_s.at[s], d_r.at[s], ba=me - 1)
+        mine = lambda s: gw[a, :, part(s)] + rb[s].astype(F32)
+
+        def to_other_core():
+            for s in range(n_ba):
+                sb[s] = gw[1 - a, :, part(s)].astype(BF)
+            for s in range(n_ba):
+                to_core(s).start()
+
+        def line(step):
+            def run():
+                if step == 0:
+                    for s in range(n_ba):
+                        to_core(s).wait_recv()
+
+                def go_up():
+                    for s in range(n_ba - 1, step, -1):
+                        if step:
+                            up(s).wait_recv()
+                        ub[s] = (mine(s) + ui[s].astype(F32) if step else mine(s)).astype(BF)
+                        up(s).start()
+
+                def go_down():
+                    for s in range(n_ba - 1 - step):
+                        if step:
+                            down(s).wait_recv()
+                        db[s] = (mine(s) + di[s].astype(F32) if step else mine(s)).astype(BF)
+                        down(s).start()
+
+                when(me == step, go_up)
+                when(me == n_ba - 1 - step, go_down)
+
+            return run
+
+        quarter = C // n_wa
+        strip = lambda q: pl.ds(pl.multiple_of(q * quarter, quarter), quarter)
+        around = lambda d: lax.rem(w + d, n_wa)
+        to_owner = lambda q: remote(pb.at[q], pi.at[w], p_s.at[q], p_r.at[w], wa=q)
+        from_peer = lambda q: remote(pb.at[q], pi.at[q], p_s.at[q], p_r.at[q], wa=q)
+        spread = lambda q: remote(gf.at[a, strip(w)], gf.at[a, strip(w)], q_s.at[q], q_r.at[w], wa=q)
+        gather = lambda q: remote(gf.at[a, strip(q)], gf.at[a, strip(q)], q_s.at[q], q_r.at[q], wa=q)
+        swap = lambda: remote(gf.at[a], gf.at[a], f_s, f_r, ha=1 - a)
+
+        def plane_sums():
+            for s in range(n_ba):
+
+                def total(s=s):
+                    value = mine(s)
+                    if s > 0:
+                        up(s).wait_recv()
+                        value = value + ui[s].astype(F32)
+                    if s < n_ba - 1:
+                        down(s).wait_recv()
+                        value = value + di[s].astype(F32)
+                    fin[...] = value
+
+                when(me == s, total)
+            for q in range(n_wa):
+                pb[q] = fin[q * quarter : (q + 1) * quarter].astype(BF)
+            for d in range(1, n_wa):
+                to_owner(around(d)).start()
+
+        def spread_sums():
+            value = fin[strip(w)]
+            for d in range(1, n_wa):
+                from_peer(around(d)).wait_recv()
+                value = value + pi[around(d)].astype(F32)
+            gf[a, strip(w)] = value.astype(BF)
+            for d in range(1, n_wa):
+                spread(around(d)).start()
+
+        def swap_cores():
+            for d in range(1, n_wa):
+                gather(around(d)).wait_recv()
+            swap().start()
+
+        to_other_core()
+        actions = [line(s) for s in range(n_ba - 1)] + [plane_sums, spread_sums, swap_cores]
 
     def ready_back(g):
         dh[1](g)
         dh[2](g)
 
     ready_back(0)
-
-    def backward(g):
-        pl.when(g + 1 < groups)(lambda: ready_back(g + 1))
-        dh[3](g)
-        widen(dzp, g, xf)
-        conv_back_group(xf, k_ref, xp, og, ig, gk, g)
-
-    loop(groups, backward)
-    gch_out[...] = jnp.sum(gch[...], axis=1)
-    gbi_out[...] = jnp.sum(gbi[...], axis=0, keepdims=True)
-    gk_out[...] = jnp.sum(gk[...], axis=1)
+    half = rows // 2
+
+    def backward(u):
+        g = u // 2
+
+        def head():
+            when(g + 1 < groups, lambda: ready_back(g + 1))
+            dh[3](g)
+            widen(dzp, g, xf)
+
+        when(u % 2 == 0, head)
+        conv_back_group(xf, ch, xp, og, ig, gk, g, (u % 2) * half, half)
+        for k, act in enumerate(actions):
+            when(u == AT[k] * 2 * groups // 12, act)
+
+    loop(2 * groups, backward)
+
+    if not inside:
+        gch_out[...] = jnp.sum(gch[...], axis=1)
+        gbi_out[...] = jnp.sum(gbi[...], axis=0, keepdims=True)
+        gk_out[...] = jnp.sum(gk[...], axis=1)
+    else:
+        gs[...] = jnp.zeros_like(gs)
+        gs[0:49] = jnp.sum(gk[...], axis=1)
+        gs[49:54] = jnp.sum(gch[...], axis=1)[:5]
+        bias = jnp.sum(gbi[...], axis=0, keepdims=True)
+        for b in range(n_ba):
+            gs[56 + b : 57 + b] = bias[:, b * C : (b + 1) * C]
+        pair = remote(gs, gs_in, t_s, t_r, ha=1 - a)
+        pair.start()
+        pair.wait_recv()
+        gp[w] = (gs[...] + gs_in[...]).astype(BF)
+        peer = lambda q: remote(gp.at[w], gp.at[w], tp_s.at[q], tp_r.at[w], wa=q)
+        peer_in = lambda q: remote(gp.at[q], gp.at[q], tp_s.at[q], tp_r.at[q], wa=q)
+        for d in range(1, n_wa):
+            peer(around(d)).start()
+        for d in range(1, n_wa):
+            peer_in(around(d)).wait_recv()
+        tot = gp[0].astype(F32)
+        for q in range(1, n_wa):
+            tot = tot + gp[q].astype(F32)
+        low = tot.astype(BF)
+        for b in range(n_ba):
+            gz_out[b] = dg(low, place(b, (C, 128), 0), 1, 0).astype(BF)
+            line_b = low.astype(F32)[56 + b : 57 + b]
+            three = jnp.concatenate([line_b[:, k * 128 : (k + 1) * 128] for k in range(3)], axis=0)
+            gz_out[b, 56:64] = jnp.concatenate([three, jnp.zeros((5, 128), F32)], axis=0).astype(BF)
+        gz[me] = gz_out[me]
+        far = lambda b: remote(gz_out.at[b], gz.at[me], tz_s.at[b], tz_r.at[me], ba=b)
+        far_in = lambda b: remote(gz_out.at[b], gz.at[b], tz_s.at[b], tz_r.at[b], ba=b)
+        beyond = lambda d: lax.rem(me + d, n_ba)
+        for d in range(1, n_ba):
+            far(beyond(d)).start()
+        swap().wait_recv()
+        swap().wait_send()
+        for d in range(1, n_ba):
+            small_to(d).wait_send()
+            w_core(lax.rem(me + d, n_ba)).wait_send()
+        for s in range(n_ba):
+            to_core(s).wait_send()
+            when((s <= me) & (me < n_ba - 1), lambda s=s: w_up_to(s, shard(a, s)).wait_send())
+            when((s >= me) & (me > 0), lambda s=s: w_dn_to(s, shard(a, s)).wait_send())
+            when(me < s, lambda s=s: up(s).wait_send())
+            when(me > s, lambda s=s: down(s).wait_send())
+        for d in range(1, n_wa):
+            to_owner(around(d)).wait_send()
+            spread(around(d)).wait_send()
+            peer(around(d)).wait_send()
+        pair.wait_send()
+        for d in range(1, n_ba):
+            far_in(beyond(d)).wait_recv()
+        for d in range(1, n_ba):
+            far(beyond(d)).wait_send()
+        value = gz[0].astype(F32)
+        for b in range(1, n_ba):
+            value = value + gz[b].astype(F32)
+        gsmall[...] = value
     loop(groups, lambda g: (xh[4](g), dh[4](g)))
 
 
-def run_main(n_wa, x, og, gate, taps, ch, bi, wi, wo):
+AT = (1, 3, 5, 7, 8, 10)
+
+
+def run_main(n_wa, n_ba, x, og, gate, *params):
     groups, rows, cols = x.shape[:3]
+    inside = n_ba == 4
     hbm = pl.BlockSpec(memory_space=pl.ANY)
     vm = pl.BlockSpec(memory_space=pltpu.VMEM)
     big = (groups, rows + 2 * R, cols + 2 * R, 8, C)
     dma = pltpu.SemaphoreType.DMA
     S = jax.ShapeDtypeStruct
+    V = pltpu.VMEM
+    out_shape = [S(x.shape, BF), S(x.shape, BF)]
+    scratch = [
+        V(big, BF), V(big, BF), V(x.shape, BF), V(big[1:], F32), V((2, rows, cols, 8, C), F32),
+        V((8, 8, C), F32), V((8, HID), F32), V((49, 8, C), F32),
+        dma((groups, 2)), dma((groups, 2)), dma((groups,)), dma((groups,)),
+        dma((groups, 2)), dma((groups, 2)), dma((groups,)), dma((groups,)),
+        dma((groups,)), dma((groups,)),
+    ]
+    if inside:
+        out_shape += [S((2, C, C), BF), S((64, 128), F32)]
+        quarter = C // n_wa
+        sh = (n_ba, C, C)
+        scratch += [V((2, C, HID), BF), V((64, C), F32), V((1, HID), F32), V((2, C, HID), F32), V((n_ba, 64, 128), BF)]
+        scratch += [dma((n_ba - 1,)), dma((n_ba,)), dma((3,))] + [dma((n_ba,))] * 5
+        scratch += [V(sh, BF)] * 6 + [V((C, C), F32), V((n_wa, quarter, C), BF), V((n_wa, quarter, C), BF)]
+        scratch += [dma((n_ba,))] * 6 + [dma((n_wa,))] * 4 + [dma, dma]
+        scratch += [V((64, C), F32), V((64, C), F32), V((n_wa, 64, C), BF), V((n_ba, 64, 128), BF), V((n_ba, 64, 128), BF)]
+        scratch += [dma, dma, dma((n_wa,)), dma((n_wa,)), dma((n_ba,)), dma((n_ba,))]
+        in_specs = [hbm, hbm, vm, hbm, hbm]
+    else:
+        out_shape += [S((2, C, HID), F32), S((8, C), F32), S((1, HID), F32), S((49, C), F32)]
+        in_specs = [hbm, hbm] + [vm] * 4
     return pl.pallas_call(
-        functools.partial(main_kernel, n_wa),
-        out_shape=(S(x.shape, BF), S(x.shape, BF), S((C, HID), F32), S((C, HID), F32), S((8, C), F32), S((1, HID), F32), S((49, C), F32)),
-        in_specs=[hbm, hbm] + [vm] * 6,
-        out_specs=(vm,) * 7,
-        scratch_shapes=[
-            pltpu.VMEM(big, BF), pltpu.VMEM(big, BF), pltpu.VMEM(x.shape, BF),
-            pltpu.VMEM(big[1:], F32), pltpu.VMEM((rows, cols, 8, C), F32),
-            pltpu.VMEM((8, 8, C), F32), pltpu.VMEM((8, HID), F32), pltpu.VMEM((49, 8, C), F32),
-            dma((groups, 2)), dma((groups, 2)), dma((groups,)), dma((groups,)),
-            dma((groups, 2)), dma((groups, 2)), dma((groups,)), dma((groups,)),
-            dma((groups,)), dma((groups,)),
-        ],
+        functools.partial(main_kernel, n_wa, n_ba),
+        out_shape=out_shape,
+        in_specs=in_specs,
+        out_specs=[vm] * len(out_shape),
+        scratch_shapes=scratch,
         compiler_params=pltpu.CompilerParams(collective_id=0, has_side_effects=True, vmem_limit_bytes=67043328),
         name="main",
-    )(x, og, gate, taps, ch, bi, wi, wo)
+    )(x, og, gate, *params)
 
 
 def adam_step(master, grad, moment, second, average, rate):
@@ -322,15 +589,9 @@
     bias_average,
 ):
     n_img, rows, cols = images.shape[0], images.shape[1], images.shape[2]
+    n_wa, n_ba = lax.axis_size("wa"), lax.axis_size("ba")
     groups = -(-n_img // 8)
     slots = groups * 8
-    mats_all, chan_all, bias_all = (
-        lax.all_gather(mats_master.astype(BF), "ba", axis=2, tiled=True),
-        lax.all_gather(chan_master.astype(BF), "ba", axis=1, tiled=True),
-        lax.all_gather(bias_master.astype(BF), "ba", axis=0, tiled=True),
-    )
-    chan_vals = chan_all.astype(F32)
-    taps, rest = chan_vals[:49], jnp.pad(chan_vals[49:], ((0, 3), (0, 0)))
     fill = jnp.arange(n_img, dtype=jnp.int32) < img_counts[0]
     gate = jnp.pad(jnp.where(fill, keep_mask, 0).astype(F32), (0, slots - n_img))
     gate = jnp.broadcast_to(gate.reshape(groups, 8, 1), (groups, 8, C))
@@ -339,21 +600,38 @@
         v = jnp.pad(v.transpose(1, 2, 0, 3), ((0, 0), (0, 0), (0, slots - n_img), (0, 0)))
         return v.reshape(rows, cols, groups, 8, C).transpose(2, 0, 1, 3, 4)
 
-    out, ig, grad_win, grad_wout, gch, gbi, grad_taps = run_main(
-        lax.axis_size("wa"), grouped(images), grouped(out_grad), gate, taps[:, None],
-        rest, bias_all.astype(F32)[None], mats_all[0], mats_all[1],
-    )
+    low = lambda v: v.astype(BF)
+    if n_ba == 4:
+        small = jnp.concatenate(
+            [
+                jnp.pad(low(chan_master), ((0, 2), (0, 32))),
+                jnp.pad(low(bias_master).reshape(3, 128), ((0, 5), (0, 0))),
+            ]
+        )
+        params = (low(mats_master), small)
+    else:
+        chan_all = lax.all_gather(low(chan_master), "ba", axis=1, tiled=True).astype(F32)
+        params = (
+            lax.all_gather(low(mats_master), "ba", axis=2, tiled=True),
+            jnp.pad(chan_all, ((0, 10), (0, 0))),
+            lax.all_gather(low(bias_master), "ba", axis=0, tiled=True).astype(F32)[None],
+        )
+    out, ig, *grads = run_main(n_wa, n_ba, grouped(images), grouped(out_grad), gate, *params)
     back = lambda v: v.transpose(1, 2, 0, 3, 4).reshape(rows, cols, slots, C)[:, :, :n_img].transpose(2, 0, 1, 3)
     outputs, input_grad = back(out), back(ig)
-    mats_local = jnp.stack([grad_win, grad_wout], axis=0)
-    chan_local = jnp.concatenate([grad_taps, gch[:5]], axis=0)
-    grad_hbias = gbi[0]
-    whole = lax.psum((mats_local, chan_local, grad_hbias), ("ha", "wa"))
-    mats_grad, chan_grad, bias_grad = (
-        lax.psum_scatter(whole[0], "ba", scatter_dimension=2, tiled=True),
-        lax.psum_scatter(whole[1], "ba", scatter_dimension=1, tiled=True),
-        lax.psum_scatter(whole[2], "ba", scatter_dimension=0, tiled=True),
-    )
+    if n_ba == 4:
+        mats_grad = grads[0].astype(F32)
+        chan_grad = grads[1][:54, :96]
+        bias_grad = grads[1][56:59].reshape(-1)
+    else:
+        whole = lax.psum(
+            (grads[0], jnp.concatenate([grads[3], grads[1][:5]], axis=0), grads[2][0]), ("ha", "wa")
+        )
+        mats_grad, chan_grad, bias_grad = (
+            lax.psum_scatter(whole[0], "ba", scatter_dimension=2, tiled=True),
+            lax.psum_scatter(whole[1], "ba", scatter_dimension=1, tiled=True),
+            lax.psum_scatter(whole[2], "ba", scatter_dimension=0, tiled=True),
+        )
     mats_new, mats_moment_new, mats_second_new, mats_average_new = adam_step(
         mats_master, mats_grad, mats_moment, mats_second, mats_average, 0.03
     )

time: 396 us -> 206 us (0.52)
  waiting for transfers between devices: 129 us -> 0 us
  blocking collectives: 67.6 us -> 0 us
  Pallas kernels: 143 us -> 180 us
  between operations: 15.3 us -> 1.47 us
  other arithmetic: 18.8 us -> 10.9 us
  local copies, waits for them, and re-layouts: 21.4 us -> 13.6 us
    psum x1 -> x0, waiting for transfers between devices: 56.1 us -> none  [local(): whole = lax.psum((mats_local, chan_local, grad_hbias), ('ha', 'wa'))]
    reduce_scatter x1 -> x0, waiting for transfers between devices: 52.8 us -> none  [local(): lax.psum_scatter(whole[0], 'ba', scatter_dimension=2, tiled=True)]
    pallas_call x1, Pallas kernels: 143 us -> 180 us  [run_main(): pl.pallas_call(functools.partial(main_kernel, n_wa, n_ba), out_shape=out_...]
    psum x1 -> x0, blocking collectives: 30.2 us -> none  [local(): whole = lax.psum((mats_local, chan_local, grad_hbias), ('ha', 'wa'))]
    all_gather x2 -> x0, blocking collectives: 27.4 us -> none  [the longest x1 14.9 us: local(): lax.all_gather(chan_master.astype(BF), 'ba', axis=1, tiled=True)]
    all_gather x1 -> x0, waiting for transfers between devices: 18.6 us -> none  [local(): lax.all_gather(mats_master.astype(BF), 'ba', axis=2, tiled=True)]
    unnamed x1 -> x0, blocking collectives: 9.89 us -> none
    unnamed x44 -> x36, local copies, waits for them, and re-layouts: 7.11 us -> 1.42 us
  transfers between devices with their start and end apart: 4 -> 0, of which waited for: 4 -> 0; matrix products, arithmetic and copies ran while one was open for 6% -> 0% of each run, Pallas kernels for 0% -> 0%
where the time goes in v3:
time: 206 us
  Pallas kernels  180 us (87%)
  local copies, waits for them, and re-layouts  13.6 us (7%)
  other arithmetic  10.9 us (5%)
    pallas_call x1, Pallas kernels, run_main(): pl.pallas_call(functools.partial(main_kernel, n_wa, n_ba), out_shape=out_...  180 us
    transpose x1, local copies, waits for them, and re-layouts, grouped(): return v.reshape(rows, cols, groups, 8, C).transpose(2, 0, 1, 3, 4)  5.58 us

profile of v3, /device:TPU:0, one launch (start us, length us, event | category | flops | bytes accessed | tf_op | source)
XLA Modules:
  0.0 206.0 jit_solution(17634772707011657479)
XLA Ops:
  1.3 0.7 fusion.6
  2.0 0.7 convert_bitcast_fusion
  2.7 0.1 broadcast_in_dim.12
  2.7 0.8 convert_element_type.35
  3.5 0.6 fusion.4.refs_4_
  4.1 0.7 broadcast_in_dim.13.refs_2_
  4.8 2.1 %convert_element_type.34.refs_3_ = bf16[2,384,384]{2,1,0:T(8,128)(2,1)} convert(f32[2,384,384]{2,1,0:T(8,128)} %param.20) | non-fusion elementwise | flops 294912 | bytes 1769472 | tf_op jit(solution)/shard_map/convert_element_type | solution.py:603
  7.0 5.6 %copy_bitcast_fusion.2 = (bf16[6,12,6,8,384]{4,3,2,1,0:T(8,128)(2,1)}, bf16[6,12,6,8,384]{4,3,2,1,0:T(8,128)(2,1)}) fusion(bf16[12,6,42,384]{3,2,1,0:T(8,128)(2,1)} %bitcast.33, bf16[12,6,42,384]{3,2,1,0:T(8,128)(2,1)} %bitcast.34), kind=kLoop, calls=%fused_computation.4 | loop fusion | bytes 9953280 | tf_op jit(solution)/shard_map/transpose | solution.py:601
  12.5 180.0 %main.1 = (bf16[6,12,6,8,384]{4,3,2,1,0:T(8,128)(2,1)}, bf16[6,12,6,8,384]{4,3,2,1,0:T(8,128)(2,1)}, bf16[2,384,384]{2,1,0:T(8,128)(2,1)}, f32[64,128]{1,0:T(8,128)}) custom-call(bf16[6,12,6,8,384]{4,3,2,1,0:T(8,128)(2,1)} %get-tuple-element.44.refs_0_, bf16[6,12,6,8,384]{4,3,2,1,0:T(8,128)(2,1)} %get-tuple-element.43.refs_1_, ...), custom_call_target="tpu_custom_call" | custom-call | tf_op jit(solution)/shard_map/main/pallas_call | solution.py:551
  192.6 2.0 copy_bitcast_fusion.1
  194.6 0.0 copy-start.16
  194.7 1.8 slice_bitcast_fusion.1
  196.5 0.6 fusion.7
  197.1 0.6 multiply_add_fusion.5
  197.7 0.6 fusion.9
  198.3 0.6 multiply_add_fusion.3
  198.9 0.3 copy_bitcast_fusion
  199.3 1.8 slice_bitcast_fusion
  201.0 0.8 copy-done.3
  201.8 0.4 copy-done.4
  202.2 0.1 copy-done.6
  202.3 2.3 %fusion.11 = (bf16[2,384,384]{2,1,0:T(8,128)(2,1)}, f32[2,384,384]{2,1,0:T(8,128)S(1)}, f32[2,384,384]{2,1,0:T(8,128)}, f32[2,384,384]{2,1,0:T(8,128)}, f32[2,384,384]{2,1,0:T(8,128)}) fusion(f32[2,384,384]{2,1,0:T(8,128)S(1)} %copy-done.1, f32[2,384,384]{2,1,0:T(8,128)S(1)} %copy-done.3, f32[2,384,384]{2,1,0:T(8,128)S(1)} %copy-done.4, ...), kind=kLoop, calls=%fused_computation.34 | loop fusion | flops 4718592 | bytes 9437184 | tf_op jit(solution)/shard_map/convert_element_type | solution.py:662
  204.6 1.3 multiply_add_fusion.1
  205.9 0.1 copy-done
  (32 shorter events, 0.1 us)
Async XLA Ops:
  194.6 1.9 copy-start.9
  194.6 1.9 copy-start.14
  194.6 1.9 copy-start.15
  194.6 1.9 copy-start.16
  194.6 2.4 %copy-start.17 = (f32[384]{0:T(512)S(1)}, f32[384]{0:T(512)}, u32[]{:S(2)}) copy-start(f32[384]{0:T(512)} %param.31) | copy-start | bytes 4612
  194.6 3.0 %copy-start.7 = (f32[54,96]{1,0:T(8,128)S(1)}, f32[54,96]{1,0:T(8,128)}, u32[]{:S(2)}) copy-start(f32[54,96]{1,0:T(8,128)} %param.21) | copy-start | bytes 62212
  194.6 3.0 %copy-start.10 = (f32[54,96]{1,0:T(8,128)S(1)}, f32[54,96]{1,0:T(8,128)}, u32[]{:S(2)}) copy-start(f32[54,96]{1,0:T(8,128)} %param.24) | copy-start | bytes 62212
  194.7 3.0 %copy-start.11 = (f32[54,96]{1,0:T(8,128)S(1)}, f32[54,96]{1,0:T(8,128)}, u32[]{:S(2)}) copy-start(f32[54,96]{1,0:T(8,128)} %param.27) | copy-start | bytes 62212
  194.7 3.6 %copy-start.12 = (f32[54,96]{1,0:T(8,128)S(1)}, f32[54,96]{1,0:T(8,128)}, u32[]{:S(2)}) copy-start(f32[54,96]{1,0:T(8,128)} %param.30) | copy-start | bytes 62212
  194.7 4.2 %copy-start.2 = (bf16[6,12,6,8,384]{4,3,2,1,0:T(8,128)(2,1)S(1)}, bf16[6,12,6,8,384]{4,3,2,1,0:T(8,128)(2,1)}, u32[]{:S(2)}) copy-start(bf16[6,12,6,8,384]{4,3,2,1,0:T(8,128)(2,1)} %get-tuple-element.25) | copy-start | bytes 7962628
  197.1 2.1 %copy-start.13 = (f32[384]{0:T(512)}, f32[384]{0:T(512)S(1)}, u32[]{:S(2)}) copy-start(f32[384]{0:T(512)S(1)} %get-tuple-element.29) | copy-start | bytes 4612
  198.3 0.9 copy-start.8
  199.2 1.8 copy-start.1
  199.2 2.6 %copy-start.3 = (f32[2,384,384]{2,1,0:T(8,128)S(1)}, f32[2,384,384]{2,1,0:T(8,128)}, u32[]{:S(2)}) copy-start(f32[2,384,384]{2,1,0:T(8,128)} %param.23) | copy-start | bytes 3538948
  199.2 2.9 %copy-start.4 = (f32[2,384,384]{2,1,0:T(8,128)S(1)}, f32[2,384,384]{2,1,0:T(8,128)}, u32[]{:S(2)}) copy-start(f32[2,384,384]{2,1,0:T(8,128)} %param.26) | copy-start | bytes 3538948
  199.2 3.1 %copy-start.6 = (bf16[2,384,384]{2,1,0:T(8,128)(2,1)S(1)}, bf16[2,384,384]{2,1,0:T(8,128)(2,1)}, u32[]{:S(2)}) copy-start(bf16[2,384,384]{2,1,0:T(8,128)(2,1)} %get-tuple-element.26) | copy-start | bytes 1769476
  202.3 2.3 %copy-start.5 = (f32[2,384,384]{2,1,0:T(8,128)S(1)}, f32[2,384,384]{2,1,0:T(8,128)}, u32[]{:S(2)}) copy-start(f32[2,384,384]{2,1,0:T(8,128)} %param.29) | copy-start | bytes 3538948
  204.6 1.4 copy-start

commit v4 on v3

--- a/solution.py
+++ b/solution.py
@@ -19,70 +19,73 @@
 MESH = pl.DeviceIdType.MESH
 
 
-def conv_group(xf, ch, z_ref):
-    rows, cols = z_ref.shape[0], z_ref.shape[1]
+def total(terms):
+    while len(terms) > 1:
+        terms = [sum(terms[i + 1 : i + 2], terms[i]) for i in range(0, len(terms), 2)]
+    return terms[0]
+
+
+def conv_group(xq, kb, cb, z_ref):
+    half, cols = z_ref.shape[0], z_ref.shape[1]
 
     def step(t, _):
-        hp = t // 3
-        c = pl.ds(pl.multiple_of((t % 3) * 128, 128), 128)
-        base = jnp.broadcast_to(ch[49:50, c], (8, 128))
-        acc = [[base] * cols for _ in range(2)]
-        for ii in range(KS + 1):
-            row = [xf[2 * hp + ii, w, :, c] for w in range(cols + KS - 1)]
-            for r in range(2):
-                i = ii - r
-                if 0 <= i < KS:
-                    for j in range(KS):
-                        tap = ch[i * KS + j : i * KS + j + 1, c]
-                        for w in range(cols):
-                            acc[r][w] = acc[r][w] + row[w + j] * tap
-        for r in range(2):
+        h = t // 3
+        c = pl.ds(pl.multiple_of((t % 3) * 256, 256), 256)
+        acc = [jnp.broadcast_to(cb[0:1, c], (8, 256))] * cols
+        for i in range(KS):
+            row = [xq[h + i, w, :, c] for w in range(cols + KS - 1)]
+            tap = [kb[i * KS + j, :, c] for j in range(KS)]
             for w in range(cols):
-                z_ref[2 * hp + r, w, :, c] = acc[r][w]
+                acc[w] = acc[w] + total([row[w + j] * tap[j] for j in range(KS)]).astype(F32)
+        for w in range(cols):
+            z_ref[h, w, :, c] = acc[w]
         return 0
 
-    lax.fori_loop(0, rows // 2 * 3, step, 0)
-
-
-def conv_back_group(df, ch, xp, og, ig, gk, g, first, count):
-    rows, cols = ig.shape[1], ig.shape[2]
+    lax.fori_loop(0, half * 3, step, 0)
+
+
+def conv_back_group(dq, kb, xm, og, ig, gk, g, first, count):
+    half, cols = ig.shape[1] // 2, ig.shape[2]
 
     def step(t, _):
-        h = first + t // 3
-        c = pl.ds(pl.multiple_of((t % 3) * 128, 128), 128)
-        x = [xp[g, h + R, w + R, :, c].astype(F32) for w in range(cols)]
-        acc = [og[g, h, w, :, c].astype(F32) for w in range(cols)]
-        for i in range(KS):
-            row = [df[h + KS - 1 - i, w, :, c] for w in range(cols + KS - 1)]
-            for j in range(KS):
-                tap = ch[i * KS + j : i * KS + j + 1, c]
-                part = None
+        h = first + t
+        for ct in range(3):
+            c = slice(ct * 256, ct * 256 + 256)
+            parts = [(h + half * (k // 3), slice(k % 3 * 128, k % 3 * 128 + 128)) for k in (2 * ct, 2 * ct + 1)]
+            pair = lambda w: jnp.concatenate([og[g, r, w, :, p].astype(F32) for r, p in parts], axis=1)
+            x = [xm[h, w, :, c] for w in range(cols)]
+            acc = [pair(w) for w in range(cols)]
+            for i in range(KS):
+                row = [dq[h + KS - 1 - i, w, :, c] for w in range(cols + KS - 1)]
+                tap = [kb[i * KS + j, :, c] for j in range(KS)]
                 for w in range(cols):
-                    d = row[w + KS - 1 - j]
-                    acc[w] = acc[w] + d * tap
-                    part = d * x[w] if part is None else part + d * x[w]
-                gk[i * KS + j, :, c] = gk[i * KS + j, :, c] + part
-        for w in range(cols):
-            ig[g, h, w, :, c] = acc[w].astype(BF)
+                    acc[w] = acc[w] + total([row[w + KS - 1 - j] * tap[j] for j in range(KS)]).astype(F32)
+                for j in range(KS):
+                    part = total([row[w + KS - 1 - j] * x[w] for w in range(cols)])
+                    gk[i * KS + j, :, c] = gk[i * KS + j, :, c] + part.astype(F32)
+            for w in range(cols):
+                for n, (r, p) in enumerate(parts):
+                    ig[g, r, w, :, p] = acc[w][:, n * 128 : n * 128 + 128].astype(BF)
         return 0
 
-    lax.fori_loop(0, count * 3, step, 0)
-
-
-def widen(src, g, dst):
+    lax.fori_loop(0, count, step, 0)
+
+
+def pack(src, g, dst, row0, col0):
+    half = src.shape[1] // 2 - R
+
     def step(t, _):
         for w in range(dst.shape[1]):
-            dst[t, w] = src[g, t, w].astype(F32)
+            dst[t, w, :, :C] = src[g, t + row0, w + col0]
+            dst[t, w, :, C:] = src[g, t + row0 + half, w + col0]
         return 0
 
     lax.fori_loop(0, dst.shape[0], step, 0)
 
 
 def gelu_pair(v):
-    t = 1.0 / (1.0 + (0.3275911 * 0.7071067811865476) * jnp.abs(v))
-    e = jnp.exp(v * v * -0.5)
-    tail = t * (0.127414796 + t * (-0.142248368 + t * (0.7107068705 + t * (-0.7265760135 + t * 0.5307027145)))) * e
-    phi = jnp.where(v > 0, 1.0 - tail, tail)
+    e = jnp.exp2(v * v * -0.7213475204444817)
+    phi = 0.5 + 0.5 * lax.erf(v * 0.7071067811865476)
     return v * phi, phi + v * e * 0.3989422804014327
 
 
@@ -91,12 +94,13 @@
 
 
 def mlp_group(z_ref, og, xp, gate_ref, w_all, bi_ref, ch_ref, out, dzp, gw, gch, gbi, g):
-    rows, cols = z_ref.shape[0], z_ref.shape[1]
+    half, cols = z_ref.shape[0], z_ref.shape[1]
+    rows = 2 * half
     m = rows * cols * 8
     flat = lambda v: v.reshape(m, C)
     cube = lambda v: v.reshape(rows, cols, 8, C)
     gain, shift, bo, ls = (ch_ref[k : k + 1] for k in range(50, 54))
-    z = flat(z_ref[...])
+    z = jnp.concatenate([z_ref[:, :, :, k * C : (k + 1) * C].reshape(m // 2, C) for k in range(2)], axis=0)
     zc = z - jnp.mean(z, axis=1, keepdims=True)
     inv = lax.rsqrt(jnp.mean(zc * zc, axis=1, keepdims=True) + 1e-6)
     xhat = zc * inv
@@ -112,12 +116,13 @@
         da = dg(db, w_all[1, :, hs], 1, 0)
         act, slope = gelu_pair(pre)
         act = act.astype(BF)
-        dpre = (da * slope).astype(BF)
+        dpre = da * slope
+        gbi[:, hs] += jnp.sum(dpre.reshape(m // 8, 8, HC), axis=0)
+        dpre = dpre.astype(BF)
         branch += dg(act, w_all[1, :, hs], 1, 1)
         dxn += dg(dpre, w_all[0, :, hs], 1, 1)
         gw[1, :, hs] += dg(db, act, 0, 0)
         gw[0, :, hs] += dg(xn, dpre, 0, 0)
-        gbi[:, hs] += jnp.sum(dpre.astype(F32).reshape(m // 8, 8, HC), axis=0)
     branch += bo
     mid = (slice(R, R + rows), slice(R, R + cols))
     out[g] = (xp[(g, *mid)].astype(F32) + cube(ls * branch) * gate).astype(BF)
@@ -218,7 +223,7 @@
         gf, gsmall = take(2)
     else:
         gw, gch_out, gbi_out, gk_out = take(4)
-    xp, dzp, og, xf, z, gch, gbi, gk = take(8)
+    xp, dzp, og, xq, xm, z, gch, gbi, gk, kb, cb = take(11)
     xcs, xcr, xrs, xrr, dcs, dcr, drs, drr, own_sem, og_sem = take(10)
     if inside:
         w_all, ch, bi, gw, s_all = take(5)
@@ -312,6 +317,10 @@
             for k in range(3):
                 bi[0:1, b * C + k * 128 : b * C + (k + 1) * 128] = part[k : k + 1]
 
+    for t in range(KS * KS):
+        kb[t] = jnp.broadcast_to(jnp.concatenate([ch[t : t + 1]] * 2, axis=1), (8, 2 * C)).astype(BF)
+    cb[...] = jnp.concatenate([ch[49:50]] * 2, axis=1)
+
     def ready(g):
         own(g).wait()
         xh[1](g)
@@ -320,8 +329,8 @@
     def conv(g):
         when(g + 1 < groups, lambda: ready(g + 1))
         xh[3](g)
-        widen(xp, g, xf)
-        conv_group(xf, ch, z.at[g % 2])
+        pack(xp, g, xq, 0, 0)
+        conv_group(xq, kb, cb, z.at[g % 2])
 
     ready(0)
     if inside:
@@ -434,7 +443,7 @@
         dh[2](g)
 
     ready_back(0)
-    half = rows // 2
+    quart = rows // 4
 
     def backward(u):
         g = u // 2
@@ -442,10 +451,11 @@
         def head():
             when(g + 1 < groups, lambda: ready_back(g + 1))
             dh[3](g)
-            widen(dzp, g, xf)
+            pack(dzp, g, xq, 0, 0)
+            pack(xp, g, xm, R, R)
 
         when(u % 2 == 0, head)
-        conv_back_group(xf, ch, xp, og, ig, gk, g, (u % 2) * half, half)
+        conv_back_group(xq, kb, xm, og, ig, gk, g, (u % 2) * quart, quart)
         for k, act in enumerate(actions):
             when(u == AT[k] * 2 * groups // 12, act)
 
@@ -454,10 +464,12 @@
     if not inside:
         gch_out[...] = jnp.sum(gch[...], axis=1)
         gbi_out[...] = jnp.sum(gbi[...], axis=0, keepdims=True)
-        gk_out[...] = jnp.sum(gk[...], axis=1)
+        both = jnp.sum(gk[...], axis=1)
+        gk_out[...] = both[:, :C] + both[:, C:]
     else:
         gs[...] = jnp.zeros_like(gs)
-        gs[0:49] = jnp.sum(gk[...], axis=1)
+        both = jnp.sum(gk[...], axis=1)
+        gs[0:49] = both[:, :C] + both[:, C:]
         gs[49:54] = jnp.sum(gch[...], axis=1)[:5]
         bias = jnp.sum(gbi[...], axis=0, keepdims=True)
         for b in range(n_ba):
@@ -528,8 +540,9 @@
     V = pltpu.VMEM
     out_shape = [S(x.shape, BF), S(x.shape, BF)]
     scratch = [
-        V(big, BF), V(big, BF), V(x.shape, BF), V(big[1:], F32), V((2, rows, cols, 8, C), F32),
-        V((8, 8, C), F32), V((8, HID), F32), V((49, 8, C), F32),
+        V(big, BF), V(big, BF), V(x.shape, BF), V((rows // 2 + 2 * R, cols + 2 * R, 8, 2 * C), BF),
+        V((rows // 2, cols, 8, 2 * C), BF), V((2, rows // 2, cols, 8, 2 * C), F32), V((8, 8, C), F32), V((8, HID), F32),
+        V((49, 8, 2 * C), F32), V((49, 8, 2 * C), BF), V((1, 2 * C), F32),
         dma((groups, 2)), dma((groups, 2)), dma((groups,)), dma((groups,)),
         dma((groups, 2)), dma((groups, 2)), dma((groups,)), dma((groups,)),
         dma((groups,)), dma((groups,)),

time: 206 us -> 175 us (0.85)
  Pallas kernels: 180 us -> 149 us
    pallas_call x1, Pallas kernels: 180 us -> 149 us  [run_main(): pl.pallas_call(functools.partial(main_kernel, n_wa, n_ba), out_shape=out_...]
where the time goes in v4:
time: 175 us
  Pallas kernels  149 us (85%)
  local copies, waits for them, and re-layouts  13.6 us (8%)
  other arithmetic  10.9 us (6%)
    pallas_call x1, Pallas kernels, run_main(): pl.pallas_call(functools.partial(main_kernel, n_wa, n_ba), out_shape=out_...  149 us
    transpose x1, local copies, waits for them, and re-layouts, grouped(): return v.reshape(rows, cols, groups, 8, C).transpose(2, 0, 1, 3, 4)  5.58 us
    transpose x2, local copies, waits for them, and re-layouts, local(): v.transpose(1, 2, 0, 3, 4).reshape(rows, cols, slots, C)[:, :, :n_img]  3.54 us

profile of v4, /device:TPU:0, one launch (start us, length us, event | category | flops | bytes accessed | tf_op | source)
XLA Modules:
  0.0 175.1 jit_solution(15662100158800599876)
XLA Ops:
  1.3 0.7 fusion.6
  2.0 0.7 convert_bitcast_fusion
  2.7 0.1 broadcast_in_dim.12
  2.7 0.8 convert_element_type.35
  3.5 0.6 fusion.4.refs_4_
  4.1 0.7 broadcast_in_dim.13.refs_2_
  4.8 2.1 %convert_element_type.34.refs_3_ = bf16[2,384,384]{2,1,0:T(8,128)(2,1)} convert(f32[2,384,384]{2,1,0:T(8,128)} %param.20) | non-fusion elementwise | flops 294912 | bytes 1769472 | tf_op jit(solution)/shard_map/convert_element_type | solution.py:616
  7.0 5.6 %copy_bitcast_fusion.2 = (bf16[6,12,6,8,384]{4,3,2,1,0:T(8,128)(2,1)}, bf16[6,12,6,8,384]{4,3,2,1,0:T(8,128)(2,1)}) fusion(bf16[12,6,42,384]{3,2,1,0:T(8,128)(2,1)} %bitcast.33, bf16[12,6,42,384]{3,2,1,0:T(8,128)(2,1)} %bitcast.34), kind=kLoop, calls=%fused_computation.4 | loop fusion | bytes 9953280 | tf_op jit(solution)/shard_map/transpose | solution.py:614
  12.5 149.1 %main.1 = (bf16[6,12,6,8,384]{4,3,2,1,0:T(8,128)(2,1)}, bf16[6,12,6,8,384]{4,3,2,1,0:T(8,128)(2,1)}, bf16[2,384,384]{2,1,0:T(8,128)(2,1)}, f32[64,128]{1,0:T(8,128)}) custom-call(bf16[6,12,6,8,384]{4,3,2,1,0:T(8,128)(2,1)} %get-tuple-element.44.refs_0_, bf16[6,12,6,8,384]{4,3,2,1,0:T(8,128)(2,1)} %get-tuple-element.43.refs_1_, ...), custom_call_target="tpu_custom_call" | custom-call | tf_op jit(solution)/shard_map/main/pallas_call | solution.py:564
  161.6 2.0 %copy_bitcast_fusion.1 = bf16[12,6,48,384]{3,2,1,0:T(8,128)(2,1)S(1)} fusion(bf16[6,12,6,8,384]{4,3,2,1,0:T(8,128)(2,1)} %get-tuple-element.24), kind=kLoop, calls=%fused_computation.3 | loop fusion | bytes 5308416 | tf_op jit(solution)/shard_map/reshape | solution.py:633
  163.7 0.0 copy-start.15
  163.8 1.8 %slice_bitcast_fusion.1 = bf16[42,12,6,384]{3,0,2,1:T(8,128)(2,1)} fusion(bf16[12,6,48,384]{3,2,1,0:T(8,128)(2,1)S(1)} %copy_bitcast_fusion.1), kind=kLoop, calls=%fused_computation.1 | loop fusion | bytes 4644864 | tf_op jit(solution)/shard_map/transpose | solution.py:633
  165.5 0.6 fusion.7
  166.1 0.6 multiply_add_fusion.5
  166.7 0.6 fusion.9
  167.4 0.6 multiply_add_fusion.3
  168.0 0.3 copy_bitcast_fusion
  168.3 1.8 %slice_bitcast_fusion = bf16[42,12,6,384]{3,0,2,1:T(8,128)(2,1)} fusion(bf16[12,6,48,384]{3,2,1,0:T(8,128)(2,1)S(1)} %copy_bitcast_fusion), kind=kLoop, calls=%fused_computation | loop fusion | bytes 4644864 | tf_op jit(solution)/shard_map/transpose | solution.py:633
  170.1 0.8 copy-done.3
  170.9 0.4 copy-done.4
  171.2 0.1 copy-done.6
  171.4 2.3 %fusion.11 = (bf16[2,384,384]{2,1,0:T(8,128)(2,1)}, f32[2,384,384]{2,1,0:T(8,128)S(1)}, f32[2,384,384]{2,1,0:T(8,128)}, f32[2,384,384]{2,1,0:T(8,128)}, f32[2,384,384]{2,1,0:T(8,128)}) fusion(f32[2,384,384]{2,1,0:T(8,128)S(1)} %copy-done.1, f32[2,384,384]{2,1,0:T(8,128)S(1)} %copy-done.3, f32[2,384,384]{2,1,0:T(8,128)S(1)} %copy-done.4, ...), kind=kLoop, calls=%fused_computation.34 | loop fusion | flops 4718592 | bytes 9437184 | tf_op jit(solution)/shard_map/convert_element_type | solution.py:675
  173.7 1.3 multiply_add_fusion.1
  175.0 0.1 copy-done
  (32 shorter events, 0.1 us)
Async XLA Ops:
  163.6 1.9 %copy-start.9 = (f32[64,128]{1,0:T(8,128)S(1)}, f32[64,128]{1,0:T(8,128)}, u32[]{:S(2)}) copy-start(f32[64,128]{1,0:T(8,128)} %get-tuple-element.27) | copy-start | bytes 98308
  163.6 1.9 %copy-start.14 = (f32[384]{0:T(512)S(1)}, f32[384]{0:T(512)}, u32[]{:S(2)}) copy-start(f32[384]{0:T(512)} %param.22) | copy-start | bytes 4612
  163.7 1.9 %copy-start.15 = (f32[384]{0:T(512)S(1)}, f32[384]{0:T(512)}, u32[]{:S(2)}) copy-start(f32[384]{0:T(512)} %param.25) | copy-start | bytes 4612
  163.7 1.9 %copy-start.16 = (f32[384]{0:T(512)S(1)}, f32[384]{0:T(512)}, u32[]{:S(2)}) copy-start(f32[384]{0:T(512)} %param.28) | copy-start | bytes 4612
  163.7 2.4 %copy-start.17 = (f32[384]{0:T(512)S(1)}, f32[384]{0:T(512)}, u32[]{:S(2)}) copy-start(f32[384]{0:T(512)} %param.31) | copy-start | bytes 4612
  163.7 3.0 %copy-start.7 = (f32[54,96]{1,0:T(8,128)S(1)}, f32[54,96]{1,0:T(8,128)}, u32[]{:S(2)}) copy-start(f32[54,96]{1,0:T(8,128)} %param.21) | copy-start | bytes 62212
  163.7 3.0 %copy-start.10 = (f32[54,96]{1,0:T(8,128)S(1)}, f32[54,96]{1,0:T(8,128)}, u32[]{:S(2)}) copy-start(f32[54,96]{1,0:T(8,128)} %param.24) | copy-start | bytes 62212
  163.7 3.0 %copy-start.11 = (f32[54,96]{1,0:T(8,128)S(1)}, f32[54,96]{1,0:T(8,128)}, u32[]{:S(2)}) copy-start(f32[54,96]{1,0:T(8,128)} %param.27) | copy-start | bytes 62212
  163.7 3.6 %copy-start.12 = (f32[54,96]{1,0:T(8,128)S(1)}, f32[54,96]{1,0:T(8,128)}, u32[]{:S(2)}) copy-start(f32[54,96]{1,0:T(8,128)} %param.30) | copy-start | bytes 62212
  163.7 4.2 %copy-start.2 = (bf16[6,12,6,8,384]{4,3,2,1,0:T(8,128)(2,1)S(1)}, bf16[6,12,6,8,384]{4,3,2,1,0:T(8,128)(2,1)}, u32[]{:S(2)}) copy-start(bf16[6,12,6,8,384]{4,3,2,1,0:T(8,128)(2,1)} %get-tuple-element.25) | copy-start | bytes 7962628
  166.1 2.1 %copy-start.13 = (f32[384]{0:T(512)}, f32[384]{0:T(512)S(1)}, u32[]{:S(2)}) copy-start(f32[384]{0:T(512)S(1)} %get-tuple-element.29) | copy-start | bytes 4612
  167.4 0.9 copy-start.8
  168.3 1.8 %copy-start.1 = (f32[2,384,384]{2,1,0:T(8,128)S(1)}, f32[2,384,384]{2,1,0:T(8,128)}, u32[]{:S(2)}) copy-start(f32[2,384,384]{2,1,0:T(8,128)} %param.20) | copy-start | bytes 3538948
  168.3 2.6 %copy-start.3 = (f32[2,384,384]{2,1,0:T(8,128)S(1)}, f32[2,384,384]{2,1,0:T(8,128)}, u32[]{:S(2)}) copy-start(f32[2,384,384]{2,1,0:T(8,128)} %param.23) | copy-start | bytes 3538948
  168.3 2.9 %copy-start.4 = (f32[2,384,384]{2,1,0:T(8,128)S(1)}, f32[2,384,384]{2,1,0:T(8,128)}, u32[]{:S(2)}) copy-start(f32[2,384,384]{2,1,0:T(8,128)} %param.26) | copy-start | bytes 3538948
  168.3 3.1 %copy-start.6 = (bf16[2,384,384]{2,1,0:T(8,128)(2,1)S(1)}, bf16[2,384,384]{2,1,0:T(8,128)(2,1)}, u32[]{:S(2)}) copy-start(bf16[2,384,384]{2,1,0:T(8,128)(2,1)} %get-tuple-element.26) | copy-start | bytes 1769476
  171.4 2.3 %copy-start.5 = (f32[2,384,384]{2,1,0:T(8,128)S(1)}, f32[2,384,384]{2,1,0:T(8,128)}, u32[]{:S(2)}) copy-start(f32[2,384,384]{2,1,0:T(8,128)} %param.29) | copy-start | bytes 3538948
  173.7 1.4 copy-start

commit v5 on v4

--- a/solution.py
+++ b/solution.py
@@ -363,35 +363,58 @@
         mine = lambda s: gw[a, :, part(s)] + rb[s].astype(F32)
 
         def to_other_core():
-            for s in range(n_ba):
+            for s in (3, 0, 2, 1):
                 sb[s] = gw[1 - a, :, part(s)].astype(BF)
-            for s in range(n_ba):
                 to_core(s).start()
 
-        def line(step):
-            def run():
-                if step == 0:
-                    for s in range(n_ba):
-                        to_core(s).wait_recv()
-
-                def go_up():
-                    for s in range(n_ba - 1, step, -1):
-                        if step:
-                            up(s).wait_recv()
-                        ub[s] = (mine(s) + ui[s].astype(F32) if step else mine(s)).astype(BF)
-                        up(s).start()
-
-                def go_down():
-                    for s in range(n_ba - 1 - step):
-                        if step:
-                            down(s).wait_recv()
-                        db[s] = (mine(s) + di[s].astype(F32) if step else mine(s)).astype(BF)
-                        down(s).start()
-
-                when(me == step, go_up)
-                when(me == n_ba - 1 - step, go_down)
-
-            return run
+        def pass_up(s):
+            up(s).wait_recv()
+            ub[s] = (mine(s) + ui[s].astype(F32)).astype(BF)
+            up(s).start()
+
+        def pass_down(s):
+            down(s).wait_recv()
+            db[s] = (mine(s) + di[s].astype(F32)).astype(BF)
+            down(s).start()
+
+        def from_ends():
+            def low():
+                for s in range(n_ba - 1, 0, -1):
+                    to_core(s).wait_recv()
+                    ub[s] = mine(s).astype(BF)
+                    up(s).start()
+                to_core(0).wait_recv()
+
+            def high():
+                for s in range(n_ba - 1):
+                    to_core(s).wait_recv()
+                    db[s] = mine(s).astype(BF)
+                    down(s).start()
+                to_core(n_ba - 1).wait_recv()
+
+            def between():
+                for s in range(n_ba):
+                    to_core(s).wait_recv()
+
+            when(me == 0, low)
+            when(me == n_ba - 1, high)
+            when((me > 0) & (me < n_ba - 1), between)
+
+        def first_pass():
+            when(me == 1, lambda: pass_up(3))
+            when(me == 2, lambda: pass_down(0))
+
+        def second_pass():
+            def at_1():
+                pass_up(2)
+                pass_down(0)
+
+            def at_2():
+                pass_down(1)
+                pass_up(3)
+
+            when(me == 1, at_1)
+            when(me == 2, at_2)
 
         quarter = C // n_wa
         strip = lambda q: pl.ds(pl.multiple_of(q * quarter, quarter), quarter)
@@ -436,7 +459,7 @@
             swap().start()
 
         to_other_core()
-        actions = [line(s) for s in range(n_ba - 1)] + [plane_sums, spread_sums, swap_cores]
+        actions = [from_ends, first_pass, second_pass, plane_sums]
 
     def ready_back(g):
         dh[1](g)
@@ -476,12 +499,14 @@
             gs[56 + b : 57 + b] = bias[:, b * C : (b + 1) * C]
         pair = remote(gs, gs_in, t_s, t_r, ha=1 - a)
         pair.start()
+        spread_sums()
         pair.wait_recv()
         gp[w] = (gs[...] + gs_in[...]).astype(BF)
         peer = lambda q: remote(gp.at[w], gp.at[w], tp_s.at[q], tp_r.at[w], wa=q)
         peer_in = lambda q: remote(gp.at[q], gp.at[q], tp_s.at[q], tp_r.at[q], wa=q)
         for d in range(1, n_wa):
             peer(around(d)).start()
+        swap_cores()
         for d in range(1, n_wa):
             peer_in(around(d)).wait_recv()
         tot = gp[0].astype(F32)
@@ -526,7 +551,7 @@
     loop(groups, lambda g: (xh[4](g), dh[4](g)))
 
 
-AT = (1, 3, 5, 7, 8, 10)
+AT = (0, 3, 5, 8)
 
 
 def run_main(n_wa, n_ba, x, og, gate, *params):

time: 175 us -> 171 us (0.977)
  Pallas kernels: 149 us -> 145 us
    pallas_call x1, Pallas kernels: 149 us -> 145 us  [run_main(): pl.pallas_call(functools.partial(main_kernel, n_wa, n_ba), out_shape=out_...]
where the time goes in v5:
time: 171 us
  Pallas kernels  145 us (85%)
  local copies, waits for them, and re-layouts  13.6 us (8%)
  other arithmetic  10.9 us (6%)
    pallas_call x1, Pallas kernels, run_main(): pl.pallas_call(functools.partial(main_kernel, n_wa, n_ba), out_shape=out_...  145 us
    transpose x1, local copies, waits for them, and re-layouts, grouped(): return v.reshape(rows, cols, groups, 8, C).transpose(2, 0, 1, 3, 4)  5.58 us
    transpose x2, local copies, waits for them, and re-layouts, local(): v.transpose(1, 2, 0, 3, 4).reshape(rows, cols, slots, C)[:, :, :n_img]  3.54 us

profile of v5, /device:TPU:0, one launch (start us, length us, event | category | flops | bytes accessed | tf_op | source)
XLA Modules:
  0.0 170.9 jit_solution(4561882213139000495)
XLA Ops:
  1.3 0.7 fusion.6
  2.0 0.7 convert_bitcast_fusion
  2.7 0.1 broadcast_in_dim.12
  2.7 0.8 convert_element_type.35
  3.5 0.6 fusion.4.refs_4_
  4.1 0.7 broadcast_in_dim.13.refs_2_
  4.8 2.1 %convert_element_type.34.refs_3_ = bf16[2,384,384]{2,1,0:T(8,128)(2,1)} convert(f32[2,384,384]{2,1,0:T(8,128)} %param.20) | non-fusion elementwise | flops 294912 | bytes 1769472 | tf_op jit(solution)/shard_map/convert_element_type | solution.py:641
  7.0 5.6 %copy_bitcast_fusion.2 = (bf16[6,12,6,8,384]{4,3,2,1,0:T(8,128)(2,1)}, bf16[6,12,6,8,384]{4,3,2,1,0:T(8,128)(2,1)}) fusion(bf16[12,6,42,384]{3,2,1,0:T(8,128)(2,1)} %bitcast.33, bf16[12,6,42,384]{3,2,1,0:T(8,128)(2,1)} %bitcast.34), kind=kLoop, calls=%fused_computation.4 | loop fusion | bytes 9953280 | tf_op jit(solution)/shard_map/transpose | solution.py:639
  12.5 144.9 %main.1 = (bf16[6,12,6,8,384]{4,3,2,1,0:T(8,128)(2,1)}, bf16[6,12,6,8,384]{4,3,2,1,0:T(8,128)(2,1)}, bf16[2,384,384]{2,1,0:T(8,128)(2,1)}, f32[64,128]{1,0:T(8,128)}) custom-call(bf16[6,12,6,8,384]{4,3,2,1,0:T(8,128)(2,1)} %get-tuple-element.44.refs_0_, bf16[6,12,6,8,384]{4,3,2,1,0:T(8,128)(2,1)} %get-tuple-element.43.refs_1_, ...), custom_call_target="tpu_custom_call" | custom-call | tf_op jit(solution)/shard_map/main/pallas_call | solution.py:589
  157.5 2.0 %copy_bitcast_fusion.1 = bf16[12,6,48,384]{3,2,1,0:T(8,128)(2,1)S(1)} fusion(bf16[6,12,6,8,384]{4,3,2,1,0:T(8,128)(2,1)} %get-tuple-element.24), kind=kLoop, calls=%fused_computation.3 | loop fusion | bytes 5308416 | tf_op jit(solution)/shard_map/reshape | solution.py:658
  159.5 0.0 copy-start.14
  159.6 1.8 %slice_bitcast_fusion.1 = bf16[42,12,6,384]{3,0,2,1:T(8,128)(2,1)} fusion(bf16[12,6,48,384]{3,2,1,0:T(8,128)(2,1)S(1)} %copy_bitcast_fusion.1), kind=kLoop, calls=%fused_computation.1 | loop fusion | bytes 4644864 | tf_op jit(solution)/shard_map/transpose | solution.py:658
  161.4 0.6 fusion.7
  162.0 0.6 multiply_add_fusion.5
  162.6 0.6 fusion.9
  163.2 0.6 multiply_add_fusion.3
  163.8 0.3 copy_bitcast_fusion
  164.2 1.8 %slice_bitcast_fusion = bf16[42,12,6,384]{3,0,2,1:T(8,128)(2,1)} fusion(bf16[12,6,48,384]{3,2,1,0:T(8,128)(2,1)S(1)} %copy_bitcast_fusion), kind=kLoop, calls=%fused_computation | loop fusion | bytes 4644864 | tf_op jit(solution)/shard_map/transpose | solution.py:658
  165.9 0.8 copy-done.3
  166.7 0.4 copy-done.4
  167.1 0.1 copy-done.6
  167.2 2.3 %fusion.11 = (bf16[2,384,384]{2,1,0:T(8,128)(2,1)}, f32[2,384,384]{2,1,0:T(8,128)S(1)}, f32[2,384,384]{2,1,0:T(8,128)}, f32[2,384,384]{2,1,0:T(8,128)}, f32[2,384,384]{2,1,0:T(8,128)}) fusion(f32[2,384,384]{2,1,0:T(8,128)S(1)} %copy-done.1, f32[2,384,384]{2,1,0:T(8,128)S(1)} %copy-done.3, f32[2,384,384]{2,1,0:T(8,128)S(1)} %copy-done.4, ...), kind=kLoop, calls=%fused_computation.34 | loop fusion | flops 4718592 | bytes 9437184 | tf_op jit(solution)/shard_map/convert_element_type | solution.py:700
  169.5 1.3 multiply_add_fusion.1
  170.8 0.1 copy-done
  (32 shorter events, 0.1 us)
Async XLA Ops:
  159.5 1.9 %copy-start.9 = (f32[64,128]{1,0:T(8,128)S(1)}, f32[64,128]{1,0:T(8,128)}, u32[]{:S(2)}) copy-start(f32[64,128]{1,0:T(8,128)} %get-tuple-element.27) | copy-start | bytes 98308
  159.5 1.9 %copy-start.14 = (f32[384]{0:T(512)S(1)}, f32[384]{0:T(512)}, u32[]{:S(2)}) copy-start(f32[384]{0:T(512)} %param.22) | copy-start | bytes 4612
  159.5 1.9 %copy-start.15 = (f32[384]{0:T(512)S(1)}, f32[384]{0:T(512)}, u32[]{:S(2)}) copy-start(f32[384]{0:T(512)} %param.25) | copy-start | bytes 4612
  159.5 1.9 %copy-start.16 = (f32[384]{0:T(512)S(1)}, f32[384]{0:T(512)}, u32[]{:S(2)}) copy-start(f32[384]{0:T(512)} %param.28) | copy-start | bytes 4612
  159.5 2.4 %copy-start.17 = (f32[384]{0:T(512)S(1)}, f32[384]{0:T(512)}, u32[]{:S(2)}) copy-start(f32[384]{0:T(512)} %param.31) | copy-start | bytes 4612
  159.5 3.0 %copy-start.7 = (f32[54,96]{1,0:T(8,128)S(1)}, f32[54,96]{1,0:T(8,128)}, u32[]{:S(2)}) copy-start(f32[54,96]{1,0:T(8,128)} %param.21) | copy-start | bytes 62212
  159.6 3.0 %copy-start.10 = (f32[54,96]{1,0:T(8,128)S(1)}, f32[54,96]{1,0:T(8,128)}, u32[]{:S(2)}) copy-start(f32[54,96]{1,0:T(8,128)} %param.24) | copy-start | bytes 62212
  159.6 3.0 %copy-start.11 = (f32[54,96]{1,0:T(8,128)S(1)}, f32[54,96]{1,0:T(8,128)}, u32[]{:S(2)}) copy-start(f32[54,96]{1,0:T(8,128)} %param.27) | copy-start | bytes 62212
  159.6 3.6 %copy-start.12 = (f32[54,96]{1,0:T(8,128)S(1)}, f32[54,96]{1,0:T(8,128)}, u32[]{:S(2)}) copy-start(f32[54,96]{1,0:T(8,128)} %param.30) | copy-start | bytes 62212
  159.6 4.2 %copy-start.2 = (bf16[6,12,6,8,384]{4,3,2,1,0:T(8,128)(2,1)S(1)}, bf16[6,12,6,8,384]{4,3,2,1,0:T(8,128)(2,1)}, u32[]{:S(2)}) copy-start(bf16[6,12,6,8,384]{4,3,2,1,0:T(8,128)(2,1)} %get-tuple-element.25) | copy-start | bytes 7962628
  162.0 2.1 %copy-start.13 = (f32[384]{0:T(512)}, f32[384]{0:T(512)S(1)}, u32[]{:S(2)}) copy-start(f32[384]{0:T(512)S(1)} %get-tuple-element.29) | copy-start | bytes 4612
  163.2 0.9 copy-start.8
  164.1 1.8 %copy-start.1 = (f32[2,384,384]{2,1,0:T(8,128)S(1)}, f32[2,384,384]{2,1,0:T(8,128)}, u32[]{:S(2)}) copy-start(f32[2,384,384]{2,1,0:T(8,128)} %param.20) | copy-start | bytes 3538948
  164.1 2.6 %copy-start.3 = (f32[2,384,384]{2,1,0:T(8,128)S(1)}, f32[2,384,384]{2,1,0:T(8,128)}, u32[]{:S(2)}) copy-start(f32[2,384,384]{2,1,0:T(8,128)} %param.23) | copy-start | bytes 3538948
  164.1 2.9 %copy-start.4 = (f32[2,384,384]{2,1,0:T(8,128)S(1)}, f32[2,384,384]{2,1,0:T(8,128)}, u32[]{:S(2)}) copy-start(f32[2,384,384]{2,1,0:T(8,128)} %param.26) | copy-start | bytes 3538948
  164.2 3.1 %copy-start.6 = (bf16[2,384,384]{2,1,0:T(8,128)(2,1)S(1)}, bf16[2,384,384]{2,1,0:T(8,128)(2,1)}, u32[]{:S(2)}) copy-start(bf16[2,384,384]{2,1,0:T(8,128)(2,1)} %get-tuple-element.26) | copy-start | bytes 1769476
  167.2 2.3 %copy-start.5 = (f32[2,384,384]{2,1,0:T(8,128)S(1)}, f32[2,384,384]{2,1,0:T(8,128)}, u32[]{:S(2)}) copy-start(f32[2,384,384]{2,1,0:T(8,128)} %param.29) | copy-start | bytes 3538948
  169.5 1.4 copy-start
